TPU v7x, 256 devices: a whole 4x4x8 slice. The times are simulated.
256 devices in a mesh: row: 16 (over z, core), col: 16 (over y, x).
Axes of the slice: x: 4, y: 4, z: 8, core: 2. Of those that a mesh axis runs over, the one named last changes fastest.
Arguments:
- tiles: bfloat16 [16, 16, 16, 512, 512], P('row', 'col'), as said below
- tile_rows: int32 [16, 16, 16], P('row', 'col'), may hold values from 0 to 11, as said below
- tile_cols: int32 [16, 16, 16], P('row', 'col'), may hold values from 0 to 11
- tile_counts: int32 [16, 16], P('row', 'col'), may hold values from 4 to 16, as said below
- sketch: bfloat16 [98304, 256], P(('row', 'col')), as said below
Outputs:
- basis: float32 [98304, 256], P(('row', 'col'))
- factor: float32 [256, 256], replicated
Inputs may be any that keep to these rules, and one draw needn't show every extreme that they name: Within one device's slots the pairs (tile_rows, tile_cols) are all different. `tile_counts`: some device uses all 16 slots in every draw. `tiles`: real valued tile entries of order one over the square root of a row's fan-in. `sketch`: real valued entries of order one.
All inputs are finite; a program needn't handle non-finite values.
Results may differ from a plain program's by a relative error of at most 0.0023.
Values may be sent and summed in bfloat16 or wider, within the bound.
A program may use at most 64 MiB of HBM per device.

v0:
```python
import jax
import jax.numpy as jnp
from jax import lax
from jax.sharding import PartitionSpec as P

BR = 12
BC = 12


def body(tiles, tile_rows, tile_cols, tile_counts, sketch):
    tile_size = tiles.shape[-1]
    sketch_width = sketch.shape[1]
    local_tiles = tiles[0, 0]
    row_ids = tile_rows[0, 0]
    col_ids = tile_cols[0, 0]
    live_count = tile_counts[0, 0]
    gathered = lax.all_gather(sketch, "col", axis=0, tiled=True)

    def transposed_step(slot_index, running):
        matrix = lax.dynamic_index_in_dim(local_tiles, slot_index, 0, keepdims=False)
        sketch_block = lax.dynamic_slice_in_dim(
            gathered, row_ids[slot_index] * tile_size, tile_size, 0
        )
        product = lax.dot_general(
            matrix, sketch_block, (((0,), (0,)), ((), ())), preferred_element_type=jnp.float32
        )
        target = col_ids[slot_index] * tile_size
        current = lax.dynamic_slice_in_dim(running, target, tile_size, 0)
        return lax.dynamic_update_slice_in_dim(running, current + product, target, 0)

    partial_cols = lax.fori_loop(
        0, live_count, transposed_step, jnp.zeros((BC * tile_size, sketch_width), jnp.float32)
    )
    shared = lax.psum_scatter(partial_cols, "row", scatter_dimension=0, tiled=True).astype(
        jnp.bfloat16
    )
    columns = lax.all_gather(shared, "row", axis=0, tiled=True)

    def forward_step(slot_index, running):
        matrix = lax.dynamic_index_in_dim(local_tiles, slot_index, 0, keepdims=False)
        column_block = lax.dynamic_slice_in_dim(
            columns, col_ids[slot_index] * tile_size, tile_size, 0
        )
        product = jnp.dot(matrix, column_block, preferred_element_type=jnp.float32)
        target = row_ids[slot_index] * tile_size
        current = lax.dynamic_slice_in_dim(running, target, tile_size, 0)
        return lax.dynamic_update_slice_in_dim(running, current + product, target, 0)

    partial_rows = lax.fori_loop(
        0, live_count, forward_step, jnp.zeros((BR * tile_size, sketch_width), jnp.float32)
    )
    owned_rows = lax.psum_scatter(partial_rows, "col", scatter_dimension=0, tiled=True)
    total_rows = BR * tile_size * lax.axis_size("row")
    local_gram = jnp.dot(
        owned_rows.T,
        owned_rows,
        precision=lax.Precision.HIGHEST,
        preferred_element_type=jnp.float32,
    )
    gram_matrix = lax.psum(local_gram, ("row", "col")) / total_rows
    cholesky_lower = jnp.linalg.cholesky(gram_matrix)
    basis_rows = lax.linalg.triangular_solve(
        cholesky_lower, owned_rows, left_side=False, lower=True, transpose_a=True
    )
    return (basis_rows, cholesky_lower.T)


def solution(mesh):
    return jax.shard_map(
        body,
        mesh=mesh,
        in_specs=(
            P("row", "col", None, None, None),
            P("row", "col", None),
            P("row", "col", None),
            P("row", "col"),
            P(("row", "col"), None),
        ),
        out_specs=(P(("row", "col"), None), P()),
        check_vma=False,
    )
```

profile of v0, /device:TPU:1, one launch (start us, length us, event | category | flops | bytes accessed | tf_op | source)
XLA Modules:
  0.0 778.7 jit_solution(2374643312332918244)
XLA Ops:
  8.0 58.4 %all-gather.3.cloned.1.call-done = bf16[6144,256]{1,0:T(8,128)(2,1)} async-done(((bf16[384,256]{1,0:T(8,128)(2,1)}), bf16[6144,256]{1,0:T(8,128)(2,1)}) %all-gather.3.cloned.1.call-update) | async-done | bytes 3145744 | tf_op jit(solution)/shard_map/all_gather | solution.py:17
  66.4 3.1 broadcast.98.clone
  69.5 29.8 %while.21 = (s32[]{:T(128)}, f32[6144,256]{1,0:T(8,128)}, s32[]{:T(128)}, s32[16]{0:T(128)S(1)}, bf16[16,512,512]{2,1,0:T(8,128)(2,1)}, /*index=5*/s32[16]{0:T(1...) while((s32[]{:T(128)}, f32[6144,256]{1,0:T(8,128)}, ...), condition=%wide.region_1.2_spmd, body=%wide.region_0.1_spmd.sunk | while | flops 134348816 | bytes 1835287 | solution.py:31
  72.9 2.4 fusion.37
  78.7 2.4 fusion.37
  84.5 2.4 fusion.37
  90.4 2.4 fusion.37
  96.2 2.4 fusion.37
  99.3 126.3 %reduce-scatter.3.cloned.1.call-done = f32[384,256]{1,0:T(8,128)} async-done(((f32[6144,256]{1,0:T(8,128)}), f32[384,256]{1,0:T(8,128)}) %reduce-scatter.3.cloned.1.call-update) | async-done | bytes 393232 | tf_op jit(solution)/shard_map/reduce_scatter | solution.py:34
  227.4 43.4 %all-gather.5.cloned.1.call-done = bf16[6144,256]{1,0:T(8,128)(2,1)} async-done(((bf16[384,256]{1,0:T(8,128)(2,1)}), bf16[6144,256]{1,0:T(8,128)(2,1)}) %all-gather.5.cloned.1.call-update) | async-done | bytes 3145744 | tf_op jit(solution)/shard_map/all_gather | solution.py:37
  270.7 3.1 broadcast.98
  273.8 28.4 %while.22 = (s32[]{:T(128)}, f32[6144,256]{1,0:T(8,128)}, s32[]{:T(128)}, s32[16]{0:T(128)S(1)}, bf16[16,512,512]{2,1,0:T(8,128)(2,1)}, /*index=5*/s32[16]{0:T(1...) while((s32[]{:T(128)}, f32[6144,256]{1,0:T(8,128)}, ...), condition=%wide.region_4.5_spmd, body=%wide.region_3.4_spmd.sunk | while | flops 134348816 | bytes 1835287 | solution.py:49
  277.0 2.4 fusion.40
  282.5 2.4 fusion.40
  288.1 2.4 fusion.40
  293.6 2.4 fusion.40
  302.3 143.8 %reduce-scatter.5.cloned.1.call-done = f32[384,256]{1,0:T(8,128)} async-done(((f32[6144,256]{1,0:T(8,128)}), f32[384,256]{1,0:T(8,128)}) %reduce-scatter.5.cloned.1.call-update) | async-done | bytes 393232 | tf_op jit(solution)/shard_map/reduce_scatter | solution.py:52
  446.1 2.7 fusion.21
  448.8 257.3 %all-reduce.3.cloned.1.call-done = f32[256,256]{0,1:T(8,128)} async-done(((f32[256,256]{0,1:T(8,128)}), f32[256,256]{0,1:T(8,128)}) %all-reduce.3.cloned.1.call-update) | async-done | bytes 262160 | tf_op jit(solution)/shard_map/psum | solution.py:60
  708.2 11.7 %cholesky.50 = f32[128,128]{1,0:T(8,128)S(1)} custom-call(f32[128,128]{1,0:T(8,128)S(1)} %cholesky.118), custom_call_target="Cholesky" | custom-call | tf_op jit(solution)/shard_map/jit(cholesky)/cholesky | solution.py:61
  720.0 9.8 %custom-call.14 = f32[1,128,128]{1,2,0:T(8,128)S(1)} custom-call(f32[1,128,128]{2,1,0:T(8,128)S(1)} %get-tuple-element.133), custom_call_target="InvertDiagBlocksLowerTriangular" | custom-call | tf_op jit(solution)/shard_map/jit(cholesky)/cholesky | solution.py:61
  730.3 11.7 %cholesky.105 = f32[128,128]{1,0:T(8,128)S(1)} custom-call(f32[128,128]{1,0:T(8,128)S(1)} %convolution_subtract_fusion.1), custom_call_target="Cholesky" | custom-call | tf_op jit(solution)/shard_map/jit(cholesky)/cholesky | solution.py:61
  744.2 4.2 while.23
  748.5 19.7 %custom-call.15 = f32[2,128,128]{1,2,0:T(8,128)S(1)} custom-call(f32[2,128,128]{2,1,0:T(8,128)S(1)} %get-tuple-element.87), custom_call_target="InvertDiagBlocksLowerTriangular" | custom-call | tf_op jit(solution)/shard_map/triangular_solve | solution.py:62
  (64 shorter events, 29.1 us)
Async XLA Ops:
  7.2 62.3 %copy-start.2 = (s32[1,1,16]{2,1,0:T(1,128)S(1)}, s32[1,1,16]{2,1,0:T(1,128)}, u32[]{:S(2)}) copy-start(s32[1,1,16]{2,1,0:T(1,128)} %param.10) | copy-start | bytes 196
  7.2 62.3 %copy-start.1 = (s32[1,1,16]{2,1,0:T(1,128)S(1)}, s32[1,1,16]{2,1,0:T(1,128)}, u32[]{:S(2)}) copy-start(s32[1,1,16]{2,1,0:T(1,128)} %param.11) | copy-start | bytes 196
  7.2 59.2 %all-gather.3.cloned.1.call-start = ((), (), s32[]{:S(2)}) async-start(), calls=%async_computation.2 | async-start | bytes 3342336 | tf_op jit(solution)/shard_map/all_gather | solution.py:17
  7.9 217.7 %reduce-scatter.3.cloned.1.call-start = ((), (), s32[]{:S(2)}) async-start(), calls=%async_computation.3 | async-start | bytes 6684672 | tf_op jit(solution)/shard_map/reduce_scatter | solution.py:34
  99.3 171.4 %all-gather.5.cloned.1.call-start = ((), (), s32[]{:S(2)}) async-start(), calls=%async_computation.4 | async-start | bytes 3342336 | tf_op jit(solution)/shard_map/all_gather | solution.py:37
  227.3 218.7 %reduce-scatter.5.cloned.1.call-start = ((), (), s32[]{:S(2)}) async-start(), calls=%async_computation.5 | async-start | bytes 6684672 | tf_op jit(solution)/shard_map/reduce_scatter | solution.py:52
  302.2 403.9 %all-reduce.3.cloned.1.call-start = ((), (), s32[]{:S(2)}) async-start(), calls=%async_computation.6 | async-start | bytes 524288 | tf_op jit(solution)/shard_map/psum | solution.py:60
  446.1 323.4 %copy-start = (f32[384,256]{1,0:T(8,128)S(1)}, f32[384,256]{1,0:T(8,128)}, u32[]{:S(2)}) copy-start(f32[384,256]{1,0:T(8,128)} %reduce-scatter.5.cloned.1.call-done) | copy-start | bytes 1179652
Sparse Core Ops, SparseCore 0:
  10.4 55.9 all-gather.2
  99.4 126.1 reduce-scatter.2
  228.0 42.6 all-gather.4
  302.3 143.6 reduce-scatter.4
  451.9 254.1 all-reduce.2
where the time goes:
time: 781 us; the launch traced here: 779 us
  waiting for transfers between devices  630 us (81%)
  other arithmetic  57.4 us (7%)
  matrix products  29.5 us (4%)
  local copies, waits for them, and re-layouts  24.7 us (3%)
  loops' own time  21.7 us (3%)
  between operations  15.3 us (2%)
    psum x1, waiting for transfers between devices, body(): gram_matrix = lax.psum(local_gram, ('row', 'col')) / total_rows  257 us
    reduce_scatter x1, waiting for transfers between devices, body(): lax.psum_scatter(partial_rows, 'col', scatter_dimension=0, tiled=True)  144 us
    reduce_scatter x1, waiting for transfers between devices, body(): lax.psum_scatter(partial_cols, 'row', scatter_dimension=0, tiled=True)  126 us
    all_gather x1, waiting for transfers between devices, body(): gathered = lax.all_gather(sketch, 'col', axis=0, tiled=True)  58.4 us
    all_gather x1, waiting for transfers between devices, body(): columns = lax.all_gather(shared, 'row', axis=0, tiled=True)  43.4 us
    another operation x6, other arithmetic, body(): cholesky_lower = jnp.linalg.cholesky(gram_matrix)  34 us
    another operation x3, other arithmetic, body(): lax.linalg.triangular_solve(cholesky_lower, owned_rows, left_side=False,...  19.7 us
  transfers between devices with their start and end apart: 5, of which 5 were waited for; matrix products, arithmetic and copies ran while one was open for 0% of the time, Pallas kernels for 0%

commit v1 on v0

v1 whole, which is shorter than its diff:
```python
import functools

import jax
import jax.numpy as jnp
from jax import lax
from jax.experimental import pallas as pl
from jax.experimental.pallas import tpu as pltpu
from jax.sharding import PartitionSpec as P

TILE = 512
K = 256
BR = 12
BC = 12
CAP = 16
SHARD = 384
FULL = 6144
ROWS = 98304
MESH = pl.DeviceIdType.MESH
HI = lax.Precision.HIGHEST
VMEM_LIMIT = 60 * 1024 * 1024


def vmem(shape, dtype):
    return pltpu.VMEM(shape, dtype)


def whole():
    return pl.BlockSpec(memory_space=pltpu.VMEM)


def flip(i, g):
    x, y = lax.rem(i, 4), lax.div(i, 4)
    if g == 0:
        return i + 1 - 2 * lax.rem(x, 2)
    if g == 1:
        return i + 3 - 2 * x
    if g == 2:
        return i + 4 - 8 * lax.rem(y, 2)
    return i + 12 - 8 * y


def greet(devices):
    barrier = pltpu.get_barrier_semaphore()
    for device in devices:
        pl.semaphore_signal(barrier, inc=1, device_id=device, device_id_type=MESH)
    pl.semaphore_wait(barrier, len(devices))


def remote(src, dst, send_sem, recv_sem, device):
    return pltpu.make_async_remote_copy(
        src_ref=src,
        dst_ref=dst,
        send_sem=send_sem,
        recv_sem=recv_sem,
        device_id=device,
        device_id_type=MESH,
    )


def rows_at(start, size, step):
    return pl.ds(pl.multiple_of(start, step), size)


AG_STREAMS = 8
AG_Q = SHARD // AG_STREAMS


def sketch_gather(shard_ref, out_ref, send_sem, recv_sem):
    row, me = lax.axis_index("row"), lax.axis_index("col")
    near = [(row, flip(me, g)) for g in range(4)]
    greet(near)
    out_ref[rows_at(me * SHARD, SHARD, SHARD), :] = shard_ref[...]
    held = [[me] for _ in range(AG_STREAMS)]
    pending = [[] for _ in range(AG_STREAMS)]
    every = []
    for step in range(4):
        for k in range(AG_STREAMS):
            g = (k + step) % 4
            for copy in pending[k]:
                copy.wait_recv()
            pending[k] = []
            for n, block in enumerate(held[k]):
                at = rows_at(block * SHARD + k * AG_Q, AG_Q, 16)
                src = shard_ref.at[pl.ds(k * AG_Q, AG_Q), :] if n == 0 else out_ref.at[at, :]
                slot = k * 15 + 2**step - 1 + n
                copy = remote(src, out_ref.at[at, :], send_sem.at[slot], recv_sem.at[slot], near[g])
                copy.start()
                pending[k].append(copy)
                every.append(copy)
            held[k] = held[k] + [flip(b, g) for b in held[k]]
    for k in range(AG_STREAMS):
        for copy in pending[k]:
            copy.wait_recv()
    for copy in every:
        copy.wait_send()


def gather_sketch(sketch):
    return pl.pallas_call(
        sketch_gather,
        out_shape=jax.ShapeDtypeStruct((FULL, K), jnp.bfloat16),
        in_specs=[whole()],
        out_specs=whole(),
        scratch_shapes=[
            pltpu.SemaphoreType.DMA((AG_STREAMS * 15,)),
            pltpu.SemaphoreType.DMA((AG_STREAMS * 15,)),
        ],
        compiler_params=pltpu.CompilerParams(
            collective_id=0, has_side_effects=True, vmem_limit_bytes=VMEM_LIMIT
        ),
        name="gather_sketch",
    )(sketch)


def tile_loop(transposed, rows_ref, cols_ref, count_ref, tile_ref, in_ref, out_ref, acc_ref):
    s = pl.program_id(0)

    @pl.when(s == 0)
    def _():
        acc_ref[...] = jnp.zeros_like(acc_ref)

    @pl.when(s < count_ref[0])
    def _():
        r, c = rows_ref[s], cols_ref[s]
        src, dst = (r, c) if transposed else (c, r)
        block = in_ref[pl.ds(pl.multiple_of(src * TILE, TILE), TILE), :]
        dims = (((0,), (0,)), ((), ())) if transposed else (((1,), (0,)), ((), ()))
        product = lax.dot_general(tile_ref[0], block, dims, preferred_element_type=jnp.float32)
        at = pl.ds(pl.multiple_of(dst * TILE, TILE), TILE)
        acc_ref[at, :] = acc_ref[at, :] + product

    @pl.when(s == CAP - 1)
    def _():
        out_ref[...] = acc_ref[...].astype(out_ref.dtype)


def tile_loop_f32(transposed, rows_ref, cols_ref, count_ref, tile_ref, in_ref, out_ref):
    s = pl.program_id(0)

    @pl.when(s == 0)
    def _():
        out_ref[...] = jnp.zeros_like(out_ref)

    @pl.when(s < count_ref[0])
    def _():
        r, c = rows_ref[s], cols_ref[s]
        src, dst = (r, c) if transposed else (c, r)
        block = in_ref[pl.ds(pl.multiple_of(src * TILE, TILE), TILE), :]
        dims = (((0,), (0,)), ((), ())) if transposed else (((1,), (0,)), ((), ()))
        product = lax.dot_general(tile_ref[0], block, dims, preferred_element_type=jnp.float32)
        at = pl.ds(pl.multiple_of(dst * TILE, TILE), TILE)
        out_ref[at, :] = out_ref[at, :] + product


def multiply(transposed, dtype, tiles, rows, cols, count, operand):
    f32 = dtype == jnp.float32
    body = tile_loop_f32 if f32 else tile_loop

    def tile_at(s, rows_ref, cols_ref, count_ref):
        return (jnp.minimum(s, count_ref[0] - 1), 0, 0)

    return pl.pallas_call(
        functools.partial(body, transposed),
        out_shape=jax.ShapeDtypeStruct((FULL, K), dtype),
        grid_spec=pltpu.PrefetchScalarGridSpec(
            num_scalar_prefetch=3,
            grid=(CAP,),
            in_specs=[
                pl.BlockSpec((1, TILE, TILE), tile_at),
                pl.BlockSpec((FULL, K), lambda *_: (0, 0), pipeline_mode=pl.Buffered(1)),
            ],
            out_specs=pl.BlockSpec((FULL, K), lambda *_: (0, 0), pipeline_mode=pl.Buffered(1)),
            scratch_shapes=[] if f32 else [vmem((FULL, K), jnp.float32)],
        ),
        compiler_params=pltpu.CompilerParams(
            dimension_semantics=("arbitrary",), vmem_limit_bytes=VMEM_LIMIT
        ),
        name="tiles_t" if transposed else "tiles_n",
    )(rows, cols, count, tiles, operand)


HALF = SHARD // 2
CHAINS = ((1, 0, 4), (-1, 1, 4), (1, 1, 3), (-1, 0, 3))


def column_exchange(
    part_ref, out_ref, pair_buf, sums, landed, pair_send, pair_recv, chain_send, chain_recv,
    own_buf, gather_send, gather_recv, twin_send, twin_recv,
):
    row, col = lax.axis_index("row"), lax.axis_index("col")
    z, core = lax.div(row, 2), lax.rem(row, 2)
    twin = (row + 1 - 2 * core, col)

    def ring(d):
        return lax.rem(z + d + 8, 8)

    side = {1: (2 * ring(1) + core, col), -1: (2 * ring(-1) + core, col)}
    greet([twin, side[1], side[-1]])

    order = []
    for t in range(1, 5):
        for direction, half, hops in CHAINS:
            if t <= hops:
                d = direction * (hops + 1 - t)
                order.append((d % 8, half))
    order += [(0, 0), (0, 1)]
    seen = []
    for item in order:
        if item not in seen:
            seen.append(item)
    pair = {}
    for n, (d, half) in enumerate(seen):
        slot = d * 2 + half
        theirs = rows_at((2 * ring(d) + 1 - core) * SHARD + half * HALF, HALF, HALF)
        pair[(d, half)] = remote(
            part_ref.at[theirs, :], pair_buf.at[slot], pair_send.at[slot], pair_recv.at[slot], twin
        )
        pair[(d, half)].start()
    done = set()

    def chip_sum(d, half):
        d = d % 8
        slot = d * 2 + half
        if (d, half) not in done:
            pair[(d, half)].wait_recv()
            done.add((d, half))
        mine = rows_at((2 * ring(d) + core) * SHARD + half * HALF, HALF, HALF)
        return part_ref[mine, :] + pair_buf[slot]

    last = {}
    sends = []
    for t in range(1, 5):
        for n, (direction, half, hops) in enumerate(CHAINS):
            if t > hops:
                continue
            slot = n * 4 + t - 1
            value = chip_sum(direction * (hops + 1 - t), half)
            if t > 1:
                last[n].wait_recv()
                value = value + landed[slot - 1]
            sums[slot] = value
            copy = remote(
                sums.at[slot], landed.at[slot], chain_send.at[slot], chain_recv.at[slot], side[direction]
            )
            copy.start()
            last[n] = copy
            sends.append(copy)

    gathers = []
    first = {}
    for half, (a, b) in ((1, (2, 1)), (0, (3, 0))):
        value = chip_sum(0, half)
        for n in (a, b):
            last[n].wait_recv()
            value = value + landed[n * 4 + CHAINS[n][2] - 1]
        own_buf[pl.ds(half * HALF, HALF), :] = value.astype(jnp.bfloat16)
        at = rows_at(row * SHARD + half * HALF, HALF, HALF)
        out_ref[at, :] = value.astype(jnp.bfloat16)
        src = own_buf.at[pl.ds(half * HALF, HALF), :]
        for n, (direction, h, hops) in enumerate(CHAINS):
            if h == half:
                copy = remote(
                    src, out_ref.at[at, :], gather_send.at[n * 4], gather_recv.at[n * 4], side[direction]
                )
                copy.start()
                first[n] = copy
                sends.append(copy)
        copy = remote(src, out_ref.at[at, :], twin_send.at[half], twin_recv.at[half], twin)
        copy.start()
        gathers.append(copy)
        sends.append(copy)
    for t in range(1, 5):
        for n in (1, 2, 0, 3):
            direction, half, hops = CHAINS[n]
            if t > hops:
                continue
            first[n].wait_recv()
            at = rows_at((2 * ring(-direction * t) + core) * SHARD + half * HALF, HALF, HALF)
            if t < hops:
                copy = remote(
                    out_ref.at[at, :], out_ref.at[at, :],
                    gather_send.at[n * 4 + t], gather_recv.at[n * 4 + t], side[direction],
                )
                copy.start()
                first[n] = copy
                sends.append(copy)
            slot = 2 + n * 4 + t - 1
            copy = remote(out_ref.at[at, :], out_ref.at[at, :], twin_send.at[slot], twin_recv.at[slot], twin)
            copy.start()
            gathers.append(copy)
            sends.append(copy)
    for copy in gathers:
        copy.wait_recv()
    for copy in sends:
        copy.wait_send()
    for item in seen:
        pair[item].wait_send()


def exchange_columns(partial):
    dma = pltpu.SemaphoreType.DMA
    return pl.pallas_call(
        column_exchange,
        out_shape=jax.ShapeDtypeStruct((FULL, K), jnp.bfloat16),
        in_specs=[whole()],
        out_specs=whole(),
        scratch_shapes=[
            vmem((16, HALF, K), jnp.float32),
            vmem((16, HALF, K), jnp.float32),
            vmem((16, HALF, K), jnp.float32),
            dma((16,)),
            dma((16,)),
            dma((16,)),
            dma((16,)),
            vmem((SHARD, K), jnp.bfloat16),
            dma((16,)),
            dma((16,)),
            dma((18,)),
            dma((18,)),
        ],
        compiler_params=pltpu.CompilerParams(
            collective_id=1, has_side_effects=True, vmem_limit_bytes=VMEM_LIMIT
        ),
        name="exchange_columns",
    )(partial)


RS_STREAMS = 8
RS_Q = SHARD // RS_STREAMS


def row_reduce(
    part_ref, ns_ref, gram_ref, land0, land1, land2, land3, acc, s0, r0, s1, r1,
    local, cols_in, col_send, col_recv, half_out, half_in, half_send, half_recv,
    z_in, z_send, z_recv, slab, out_send, out_recv,
):
    row, me = lax.axis_index("row"), lax.axis_index("col")
    z, core = lax.div(row, 2), lax.rem(row, 2)
    other = row + 1 - 2 * core
    twin = (other, me)
    near = [(row, flip(me, g)) for g in range(4)]
    plane = [lax.rem(me + d, 16) for d in range(1, 16)]
    column = [2 * lax.rem(z + d, 8) + core for d in range(1, 8)]
    greet(
        [(row, p) for p in plane] + [(other, p) for p in plane] + [twin] + [(q, me) for q in column]
    )
    sends = []

    combos = [(a, b, c) for a in (0, 1) for b in (0, 1) for c in (0, 1)]
    waits = {}

    def moved(k, combo):
        block = me
        for bit, i in zip(combo, (1, 2, 3)):
            if bit:
                block = flip(block, (k + i) % 4)
        return block

    for k in range(RS_STREAMS):
        copies = []
        for n, combo in enumerate(combos):
            block = flip(moved(k, combo), k % 4)
            at = rows_at(block * SHARD + k * RS_Q, RS_Q, 16)
            slot = k * 8 + n
            copy = remote(part_ref.at[at, :], land0.at[slot], s0.at[slot], r0.at[slot], near[k % 4])
            copy.start()
            copies.append(copy)
        waits[k] = copies
        sends += copies
    lands = {1: land1, 2: land2, 3: land3}
    for step in range(1, 5):
        for k in range(RS_STREAMS):
            size = 2 ** (4 - step)
            for copy in waits[k]:
                copy.wait_recv()
            if step == 1:
                for n in range(size - 1, -1, -1):
                    at = rows_at(moved(k, combos[n]) * SHARD + k * RS_Q, RS_Q, 16)
                    slot = k * 8 + n
                    acc[slot] = part_ref[at, :].astype(jnp.float32) + land0[slot].astype(jnp.float32)
            else:
                land = lands[step - 1]
                for n in range(size):
                    acc[k * 8 + n] = acc[k * 8 + n] + land[k * size + n].astype(jnp.float32)
            if step < 4:
                half = size // 2
                slot = k * 3 + step - 1
                copy = remote(
                    acc.at[pl.ds(k * 8 + half, half)],
                    lands[step].at[pl.ds(k * half, half)],
                    s1.at[slot],
                    r1.at[slot],
                    near[(k + step) % 4],
                )
                copy.start()
                waits[k] = [copy]
                sends.append(copy)
            else:
                ns_ref[pl.ds(k * RS_Q, RS_Q), :] = acc[k * 8]

    rows = ns_ref[...]
    local[...] = lax.dot_general(
        rows, rows, (((0,), (0,)), ((), ())), precision=HI, preferred_element_type=jnp.float32
    )
    copies = []
    for d, p in enumerate(plane):
        copy = remote(
            local.at[rows_at(p * 16, 16, 16), :], cols_in.at[d], col_send.at[d], col_recv.at[d], (row, p)
        )
        copy.start()
        copies.append(copy)
    sends += copies
    total = local[rows_at(me * 16, 16, 16), :]
    for d, copy in enumerate(copies):
        copy.wait_recv()
        total = total + cols_in[d]
    half_out[...] = total
    copy = remote(half_out.at[rows_at((1 - core) * 8, 8, 8), :], half_in, half_send, half_recv, twin)
    copy.start()
    copy.wait_recv()
    sends.append(copy)
    slab[...] = half_out[rows_at(core * 8, 8, 8), :] + half_in[...]
    copies = []
    for d, q in enumerate(column):
        copy = remote(slab, z_in.at[z], z_send.at[d], z_recv.at[d], (q, me))
        copy.start()
        copies.append(copy)
    sends += copies
    z_in[z] = slab[...]
    for copy in copies:
        copy.wait_recv()
    total = z_in[0]
    for d in range(1, 8):
        total = total + z_in[d]
    at = rows_at(me * 16 + core * 8, 8, 8)
    gram_ref[at, :] = total * (1.0 / ROWS)
    copies = []
    for n, device in enumerate([twin] + [(r, p) for p in plane for r in (row, other)]):
        copy = remote(gram_ref.at[at, :], gram_ref.at[at, :], out_send.at[n], out_recv.at[n], device)
        copy.start()
        copies.append(copy)
    for copy in copies:
        copy.wait_recv()
    for copy in sends + copies:
        copy.wait_send()


def reduce_rows(partial):
    dma = pltpu.SemaphoreType.DMA
    f32 = jnp.float32
    n = RS_STREAMS
    return pl.pallas_call(
        row_reduce,
        out_shape=(
            jax.ShapeDtypeStruct((SHARD, K), f32),
            jax.ShapeDtypeStruct((K, K), f32),
        ),
        in_specs=[whole()],
        out_specs=(whole(), whole()),
        scratch_shapes=[
            vmem((n * 8, RS_Q, K), partial.dtype),
            vmem((n * 4, RS_Q, K), f32),
            vmem((n * 2, RS_Q, K), f32),
            vmem((n, RS_Q, K), f32),
            vmem((n * 8, RS_Q, K), f32),
            dma((n * 8,)),
            dma((n * 8,)),
            dma((n * 3,)),
            dma((n * 3,)),
            vmem((K, K), f32),
            vmem((15, 16, K), f32),
            dma((15,)),
            dma((15,)),
            vmem((16, K), f32),
            vmem((8, K), f32),
            dma,
            dma,
            vmem((8, 8, K), f32),
            dma((7,)),
            dma((7,)),
            vmem((8, K), f32),
            dma((31,)),
            dma((31,)),
        ],
        compiler_params=pltpu.CompilerParams(
            collective_id=2, has_side_effects=True, vmem_limit_bytes=VMEM_LIMIT
        ),
        name="reduce_rows",
    )(partial)


OUTER = 64


def factor_kernel(gram_ref, ns_ref, basis_ref, factor_ref, work):
    i0 = lax.broadcasted_iota(jnp.int32, (K, K), 0)
    i1 = lax.broadcasted_iota(jnp.int32, (K, K), 1)
    work[:, :K] = gram_ref[...]
    work[:, K:] = (i0 == i1).astype(jnp.float32)
    sub = lax.broadcasted_iota(jnp.int32, (8, 128), 0)
    for o in range(K // OUTER):
        base = o * OUTER
        for p in range(OUTER // 8):
            j = base + p * 8
            panel = work[pl.ds(j, 8), :]
            if p:
                done = work[pl.ds(base, p * 8), :]
                panel = panel - lax.dot_general(
                    done[:, j : j + 8], done, (((0,), (0,)), ((), ())),
                    precision=HI, preferred_element_type=jnp.float32,
                )
            parts = [panel[:, q * 128 : (q + 1) * 128] for q in range(4)]
            cols = [jnp.broadcast_to(panel[:, j + k : j + k + 1], (8, 128)) for k in range(8)]
            for i in range(8):
                scale = lax.rsqrt(jnp.broadcast_to(cols[i][i : i + 1, :], (8, 128)))
                down = jnp.where(sub > i, cols[i] * scale, 0.0)
                for k in range(i + 1, 8):
                    cols[k] = cols[k] - down * (jnp.broadcast_to(cols[k][i : i + 1, :], (8, 128)) * scale)
                for q in range(4):
                    line = jnp.broadcast_to(parts[q][i : i + 1, :], (8, 128)) * scale
                    parts[q] = jnp.where(sub == i, line, parts[q] - down * line)
            for q in range(4):
                work[pl.ds(j, 8), q * 128 : (q + 1) * 128] = parts[q]
        rest = K - base - OUTER
        if rest:
            done = work[pl.ds(base, OUTER), :]
            work[pl.ds(base + OUTER, rest), :] = work[pl.ds(base + OUTER, rest), :] - lax.dot_general(
                done[:, base + OUTER : K], done, (((0,), (0,)), ((), ())),
                precision=HI, preferred_element_type=jnp.float32,
            )
    factor_ref[...] = jnp.where(i1 >= i0, work[:, :K], 0.0)
    inverse_t = jnp.where(i0 >= i1, work[:, K:], 0.0)
    basis_ref[...] = lax.dot_general(
        ns_ref[...], inverse_t, (((1,), (1,)), ((), ())), precision=HI, preferred_element_type=jnp.float32
    )


def factor_and_basis(gram, ns):
    return pl.pallas_call(
        factor_kernel,
        out_shape=(
            jax.ShapeDtypeStruct((SHARD, K), jnp.float32),
            jax.ShapeDtypeStruct((K, K), jnp.float32),
        ),
        in_specs=[whole(), whole()],
        out_specs=(whole(), whole()),
        scratch_shapes=[vmem((K, 2 * K), jnp.float32)],
        compiler_params=pltpu.CompilerParams(vmem_limit_bytes=VMEM_LIMIT),
        name="factor",
    )(gram, ns)


def body(tiles, tile_rows, tile_cols, tile_counts, sketch):
    local_tiles = tiles[0, 0]
    rows, cols, count = tile_rows[0, 0], tile_cols[0, 0], tile_counts[0]
    gathered = gather_sketch(sketch)
    partial_cols = multiply(True, jnp.float32, local_tiles, rows, cols, count, gathered)
    columns = exchange_columns(partial_cols)
    partial_rows = multiply(False, jnp.bfloat16, local_tiles, rows, cols, count, columns)
    ns, gram = reduce_rows(partial_rows)
    return factor_and_basis(gram, ns)


def solution(mesh):
    return jax.shard_map(
        body,
        mesh=mesh,
        in_specs=(
            P("row", "col", None, None, None),
            P("row", "col", None),
            P("row", "col", None),
            P("row", "col"),
            P(("row", "col"), None),
        ),
        out_specs=(P(("row", "col"), None), P()),
        check_vma=False,
    )
```

time: 781 us -> 199 us (0.25)
  waiting for transfers between devices: 630 us -> 0 us
  Pallas kernels: 0 us -> 198 us
  other arithmetic: 57.4 us -> 0 us
  matrix products: 29.5 us -> 0 us
  local copies, waits for them, and re-layouts: 24.7 us -> 0 us
  loops' own time: 21.7 us -> 0 us
  between operations: 15.3 us -> 1.3 us
    reduce_scatter x2 -> x0, waiting for transfers between devices: 270 us -> none  [the longest x1 144 us: body(): lax.psum_scatter(partial_rows, 'col', scatter_dimension=0, tiled=True)]
    psum x1 -> x0, waiting for transfers between devices: 257 us -> none  [body(): gram_matrix = lax.psum(local_gram, ('row', 'col')) / total_rows]
    pallas_call x0 -> x6, Pallas kernels: none -> 198 us  [the longest x1 68.1 us: exchange_columns(): pl.pallas_call(column_exchange, out_shape=jax.ShapeDtypeStruct((FULL, K),...]
    all_gather x2 -> x0, waiting for transfers between devices: 102 us -> none  [the longest x1 58.4 us: body(): gathered = lax.all_gather(sketch, 'col', axis=0, tiled=True)]
    another operation x9 -> x0, other arithmetic: 53.7 us -> none  [the longest x6 34 us: body(): cholesky_lower = jnp.linalg.cholesky(gram_matrix)]
    dot_general x11 -> x0, matrix products: 26.8 us -> none  [the longest x5 12.2 us: transposed_step(): lax.dot_general(matrix, sketch_block, (((0,), (0,)), ((), ())), preferred...]
    another operation x3 -> x0, loops' own time: 21.7 us -> none  [the longest x1 11 us: body(): lax.fori_loop(0, live_count, transposed_step, jnp.zeros((BC * tile_size,...]
    dynamic_slice x20 -> x0, local copies, waits for them, and re-layouts: 12.5 us -> none  [the longest x5 3.32 us: transposed_step(): target = col_ids[slot_index] * tile_size]
  transfers between devices with their start and end apart: 5 -> 0, of which waited for: 5 -> 0; matrix products, arithmetic and copies ran while one was open for 0% -> 0% of each run, Pallas kernels for 0% -> 0%
where the time goes in v1:
time: 199 us
  Pallas kernels  198 us (99%)
    pallas_call x1, Pallas kernels, exchange_columns(): pl.pallas_call(column_exchange, out_shape=jax.ShapeDtypeStruct((FULL, K),...  68.1 us
    pallas_call x1, Pallas kernels, reduce_rows(): pl.pallas_call(row_reduce, out_shape=(jax.ShapeDtypeStruct((SHARD, K), f3...  58.9 us
    pallas_call x1, Pallas kernels, gather_sketch(): pl.pallas_call(sketch_gather, out_shape=jax.ShapeDtypeStruct((FULL, K), j...  30 us
    pallas_call x2, Pallas kernels, multiply(): pl.pallas_call(functools.partial(body, transposed), out_shape=jax.ShapeDt...  23.3 us
    pallas_call x1, Pallas kernels, factor_and_basis(): pl.pallas_call(factor_kernel, out_shape=(jax.ShapeDtypeStruct((SHARD, K),...  17.2 us

profile of v1, /device:TPU:1, one launch (start us, length us, event | category | flops | bytes accessed | tf_op | source)
XLA Modules:
  0.0 198.8 jit_solution(10211036393672187311)
XLA Ops:
  1.3 30.0 %gather_sketch.1.in_ref = bf16[6144,256]{1,0:T(8,128)(2,1)} custom-call(bf16[384,256]{1,0:T(8,128)(2,1)} %shard_ref.1), custom_call_target="tpu_custom_call" | custom-call | tf_op jit(solution)/shard_map/gather_sketch/pallas_call | solution.py:99
  31.3 12.1 %tiles_t.1.part_ref = f32[6144,256]{1,0:T(8,128)} custom-call(s32[16]{0:T(128)} %bitcast.8, s32[16]{0:T(128)} %bitcast.10, s32[1]{0:T(128)} %bitcast.4.count_ref, bf16[16,512,512]{2,1,0:T(8,128)(2,1)} %bitcast.6, bf16[6144,256]{1,0:T(8,128)(2,1)} %gather_sketch.1.in_ref), custom_call_target="tpu_custom_call" | custom-call | tf_op jit(solution)/shard_map/tiles_t/pallas_call | solution.py:162
  43.4 68.1 %exchange_columns.1.in_ref = bf16[6144,256]{1,0:T(8,128)(2,1)} custom-call(f32[6144,256]{1,0:T(8,128)} %tiles_t.1.part_ref), custom_call_target="tpu_custom_call" | custom-call | tf_op jit(solution)/shard_map/exchange_columns/pallas_call | solution.py:302
  111.6 11.2 %tiles_n.1.part_ref = bf16[6144,256]{1,0:T(8,128)(2,1)} custom-call(s32[16]{0:T(128)} %bitcast.9, s32[16]{0:T(128)} %bitcast.11, s32[1]{0:T(128)} %bitcast.5.count_ref, bf16[16,512,512]{2,1,0:T(8,128)(2,1)} %bitcast.7, bf16[6144,256]{1,0:T(8,128)(2,1)} %exchange_columns.1.in_ref), custom_call_target="tpu_custom_call" | custom-call | tf_op jit(solution)/shard_map/tiles_n/pallas_call | solution.py:162
  122.8 58.9 %reduce_rows.1 = (f32[384,256]{1,0:T(8,128)}, f32[256,256]{1,0:T(8,128)}) custom-call(bf16[6144,256]{1,0:T(8,128)(2,1)} %tiles_n.1.part_ref), custom_call_target="tpu_custom_call" | custom-call | tf_op jit(solution)/shard_map/reduce_rows/pallas_call | solution.py:452
  181.6 17.2 %factor.1 = (f32[384,256]{1,0:T(8,128)}, f32[256,256]{1,0:T(8,128)}) custom-call(f32[256,256]{1,0:T(8,128)} %get-tuple-element.4.gram_ref, f32[384,256]{1,0:T(8,128)} %get-tuple-element.5.ns_ref), custom_call_target="tpu_custom_call" | custom-call | tf_op jit(solution)/shard_map/factor/pallas_call | solution.py:539

commit v2 on v0

v2 whole, which is shorter than its diff:
```python
import functools
import heapq

import jax
import jax.numpy as jnp
from jax import lax
from jax.experimental import pallas as pl
from jax.experimental.pallas import tpu as pltpu
from jax.sharding import PartitionSpec as P

TILE = 512
K = 256
H = 128
BR = 12
BC = 12
CAP = 16
SHARD = 384
HALF = SHARD // 2
FULL = 6144
UNIT = 32
TU = TILE // UNIT
HU = 192 // UNIT
ROWS = 98304
STREAMS = 4
Q = SHARD // STREAMS
MESH = pl.DeviceIdType.MESH
HI = lax.Precision.HIGHEST
VMEM_LIMIT = 60 * 1024 * 1024
F32 = jnp.float32
BF16 = jnp.bfloat16
CHAINS = ((1, 0, 4), (-1, 1, 4), (1, 1, 3), (-1, 0, 3))
WIRE = (BF16, F32, F32, F32)


def vmem(shape, dtype):
    return pltpu.VMEM(shape, dtype)


def dma(n):
    return pltpu.SemaphoreType.DMA((n,))


def whole():
    return pl.BlockSpec(memory_space=pltpu.VMEM)


def flip(i, g):
    x, y = lax.rem(i, 4), lax.div(i, 4)
    if g == 0:
        return i + 1 - 2 * lax.rem(x, 2)
    if g == 1:
        return i + 3 - 2 * x
    if g == 2:
        return i + 4 - 8 * lax.rem(y, 2)
    return i + 12 - 8 * y


def rows_at(start, size, step):
    return pl.ds(pl.multiple_of(start, step), size)


def remote(src, dst, send_sem, recv_sem, device):
    return pltpu.make_async_remote_copy(
        src_ref=src,
        dst_ref=dst,
        send_sem=send_sem,
        recv_sem=recv_sem,
        device_id=device,
        device_id_type=MESH,
    )


def last_step(mask):
    return mask.bit_length() - 1


def first_step(mask):
    return (mask & -mask).bit_length() - 1


def interleave(processes):
    queue = []
    for n, process in enumerate(processes):
        heapq.heappush(queue, (next(process), n, process))
    while queue:
        _, n, process = heapq.heappop(queue)
        try:
            heapq.heappush(queue, (next(process), n, process))
        except StopIteration:
            pass


HALF_SCRATCH = dict(
    shard=lambda: vmem((SHARD // UNIT, UNIT, H), BF16),
    gathered=lambda: vmem((FULL // UNIT, UNIT, H), BF16),
    ag_send=lambda: dma(STREAMS * 15),
    ag_recv=lambda: dma(STREAMS * 15),
    acc=lambda: vmem((CAP + 1, TILE, H), F32),
    part=lambda: vmem((FULL, H), F32),
    pair_buf=lambda: vmem((16, HALF, H), F32),
    sums=lambda: vmem((16, HALF, H), F32),
    landed=lambda: vmem((16, HALF, H), F32),
    pair_send=lambda: dma(16),
    pair_recv=lambda: dma(16),
    chain_send=lambda: dma(16),
    chain_recv=lambda: dma(16),
    own=lambda: vmem((SHARD // UNIT, UNIT, H), BF16),
    columns=lambda: vmem((FULL // UNIT, UNIT, H), BF16),
    gather_send=lambda: dma(16),
    gather_recv=lambda: dma(16),
    twin_send=lambda: dma(18),
    twin_recv=lambda: dma(18),
    part2=lambda: vmem((FULL, H), BF16),
    land0=lambda: vmem((STREAMS * 8, Q, H), BF16),
    land1=lambda: vmem((STREAMS * 4, Q, H), WIRE[1]),
    land2=lambda: vmem((STREAMS * 3, Q, H), F32),
    acc2=lambda: vmem((STREAMS * 8, Q, H), F32),
    wire1=lambda: vmem((STREAMS * 4, Q, H), BF16),
    rs_send=lambda: dma(STREAMS * 15),
    rs_recv=lambda: dma(STREAMS * 15),
)

SHARED_SCRATCH = dict(
    tiles=lambda: vmem((CAP, TILE, TILE), BF16),
    tile_sem=lambda: dma(CAP),
    gram_part=lambda: vmem((K, K), F32),
    slabs=lambda: vmem((31, 8, K), F32),
    slab=lambda: vmem((8, K), F32),
    slab_send=lambda: dma(31),
    slab_recv=lambda: dma(31),
    z_in=lambda: vmem((8, 8, K), F32),
    z_send=lambda: dma(7),
    z_recv=lambda: dma(7),
    out_send=lambda: dma(31),
    out_recv=lambda: dma(31),
)


class Refs:
    pass


def named(names, refs):
    out = Refs()
    for name, ref in zip(names, refs):
        setattr(out, name, ref)
    return out


def iterate(plan_ref, tiles_ref, sketch_ref, ns_ref, gram_ref, *scratch):
    nh = len(HALF_SCRATCH)
    halves = [named(HALF_SCRATCH, scratch[i * nh : (i + 1) * nh]) for i in (0, 1)]
    shared = named(SHARED_SCRATCH, scratch[2 * nh :])

    row, me = lax.axis_index("row"), lax.axis_index("col")
    z, core = lax.div(row, 2), lax.rem(row, 2)
    other = row + 1 - 2 * core
    twin = (other, me)
    near = [(row, flip(me, g)) for g in range(4)]
    plane = [lax.rem(me + d, 16) for d in range(1, 16)]

    def ring(d):
        return lax.rem(z + d + 8, 8)

    side = {1: (2 * ring(1) + core, me), -1: (2 * ring(-1) + core, me)}
    column = [(2 * ring(d) + core, me) for d in range(1, 8)]
    everyone = [twin] + [(r, p) for p in plane for r in (row, other)]

    loads = []
    for s in range(CAP):
        load = pltpu.make_async_copy(tiles_ref.at[s], shared.tiles.at[s], shared.tile_sem.at[s])
        load.start()
        loads.append(load)
    for i, half in enumerate(halves):
        half.shard[...] = sketch_ref[:, i * H : (i + 1) * H].reshape(SHARD // UNIT, UNIT, H)

    barrier = pltpu.get_barrier_semaphore()
    for device in everyone + column:
        pl.semaphore_signal(barrier, inc=1, device_id=device, device_id_type=MESH)
    pl.semaphore_wait(barrier, len(everyone) + len(column))

    sends = []

    def gather(half, start, flow):
        copies = {}
        half.gathered[pl.ds(me * (SHARD // UNIT), SHARD // UNIT)] = half.shard[...]

        def block_at(k, mask):
            block = me
            for s in range(4):
                if mask >> s & 1:
                    block = flip(block, (k + s) % 4)
            return pl.ds(block * (SHARD // UNIT) + k * (Q // UNIT), Q // UNIT)

        def forward(k, mask, s):
            at = block_at(k, mask)
            src = half.shard.at[pl.ds(k * (Q // UNIT), Q // UNIT)] if mask == 0 else half.gathered.at[at]
            slot = k * 15 + (mask | 1 << s) - 1
            copy = remote(
                src, half.gathered.at[at], half.ag_send.at[slot], half.ag_recv.at[slot], near[(k + s) % 4]
            )
            copy.start()
            copies[k, mask | 1 << s] = copy
            sends.append(copy)

        for s in range(4):
            for k in range(STREAMS):
                forward(k, 0, s)
        masks = sorted(range(1, 16), key=lambda m: (m.bit_count(), last_step(m), m))
        n = 0
        for mask in masks:
            for k in range(STREAMS):
                yield start + 2 + flow * n / 60
                n += 1
                copies[k, mask].wait_recv()
                for s in range(last_step(mask) + 1, 4):
                    forward(k, mask, s)

    def multiply(half, transposed, source, result, start, per_tile):
        base = 0 if transposed else PLAN
        dims = (((0,), (0,)), ((), ())) if transposed else (((1,), (0,)), ((), ()))
        for s in range(CAP):
            yield start + per_tile * s
            if loads[s] is not None:
                loads[s].wait()
                loads[s] = None
            block = source[pl.ds(plan_ref[base + s] * TU, TU)].reshape(TILE, H)
            for u in range(2):
                part = pl.ds(u * 256, 256)
                tile = shared.tiles[s, :, part] if transposed else shared.tiles[s, part, :]
                half.acc[s + 1, part, :] = half.acc[plan_ref[base + CAP + s], part, :] + lax.dot_general(
                    tile, block, dims, preferred_element_type=F32
                )
        for b in range(BR):
            yield start + per_tile * CAP + 0.08 * b
            result[pl.ds(b * TILE, TILE), :] = half.acc[plan_ref[base + 2 * CAP + b]].astype(result.dtype)

    def exchange(half, start, ring_start, reduce_flow, gather_flow):
        yield start
        order = []
        for t in range(1, 5):
            for direction, part, hops in CHAINS:
                if t <= hops:
                    item = (direction * (hops + 1 - t) % 8, part)
                    if item not in order:
                        order.append(item)
        order += [(0, 0), (0, 1)]
        pair = {}
        for d, part in order:
            slot = d * 2 + part
            theirs = rows_at((2 * ring(d) + 1 - core) * SHARD + part * HALF, HALF, HALF)
            pair[d, part] = remote(
                half.part.at[theirs, :], half.pair_buf.at[slot],
                half.pair_send.at[slot], half.pair_recv.at[slot], twin,
            )
            pair[d, part].start()
            sends.append(pair[d, part])
        arrived = set()

        def chip_sum(d, part):
            d = d % 8
            slot = d * 2 + part
            if (d, part) not in arrived:
                pair[d, part].wait_recv()
                arrived.add((d, part))
            mine = rows_at((2 * ring(d) + core) * SHARD + part * HALF, HALF, HALF)
            return half.part[mine, :] + half.pair_buf[slot]

        last = {}
        n_sent = 0
        for t in range(1, 5):
            for n, (direction, part, hops) in enumerate(CHAINS):
                if t > hops:
                    continue
                yield ring_start + 2 + reduce_flow * n_sent / 14
                n_sent += 1
                slot = n * 4 + t - 1
                value = chip_sum(direction * (hops + 1 - t), part)
                if t > 1:
                    last[n].wait_recv()
                    value = value + half.landed[slot - 1]
                half.sums[slot] = value
                copy = remote(
                    half.sums.at[slot], half.landed.at[slot],
                    half.chain_send.at[slot], half.chain_recv.at[slot], side[direction],
                )
                copy.start()
                last[n] = copy
                sends.append(copy)
        begin = ring_start + 4 + reduce_flow
        twins = []
        moving = {}

        def spread(src, at, slot):
            copy = remote(src, half.columns.at[at], half.twin_send.at[slot], half.twin_recv.at[slot], twin)
            copy.start()
            twins.append(copy)
            sends.append(copy)

        def pass_on(src, at, n, t):
            slot = n * 4 + t
            copy = remote(
                src, half.columns.at[at],
                half.gather_send.at[slot], half.gather_recv.at[slot], side[CHAINS[n][0]],
            )
            copy.start()
            moving[n] = copy
            sends.append(copy)

        for part, (a, b) in ((1, (2, 1)), (0, (3, 0))):
            yield begin
            value = chip_sum(0, part)
            for n in (a, b):
                last[n].wait_recv()
                value = value + half.landed[n * 4 + CHAINS[n][2] - 1]
            local = pl.ds(part * HU, HU)
            rounded = value.astype(BF16).reshape(HU, UNIT, H)
            half.own[local] = rounded
            at = pl.ds((row * 2 + part) * HU, HU)
            half.columns[at] = rounded
            for n in range(4):
                if CHAINS[n][1] == part:
                    pass_on(half.own.at[local], at, n, 0)
            spread(half.own.at[local], at, part)
        n_got = 0
        for t in range(1, 5):
            for n in (1, 2, 0, 3):
                direction, part, hops = CHAINS[n]
                if t > hops:
                    continue
                yield begin + 2 + gather_flow * n_got / 14
                n_got += 1
                moving[n].wait_recv()
                at = pl.ds(((2 * ring(-direction * t) + core) * 2 + part) * HU, HU)
                if t < hops:
                    pass_on(half.columns.at[at], at, n, t)
                spread(half.columns.at[at], at, 2 + n * 4 + t - 1)
        for copy in twins:
            yield begin + 3 + gather_flow
            copy.wait_recv()

    def reduce(half, lane, start, flow):
        yield start
        copies = {}

        def block_at(k, mask):
            block = me
            for s in range(4):
                if mask >> s & 1:
                    block = flip(block, (k + s) % 4)
            return rows_at(block * SHARD + k * Q, Q, 16)

        def landing(k, s, mask):
            if s == 0:
                return half.land0.at[k * 8 + mask // 2]
            if s == 1:
                return half.land1.at[k * 4 + mask // 4]
            return half.land2.at[k * 3 + (mask // 8 if s == 2 else 2)]

        def send(k, mask):
            s = first_step(mask)
            if s == 0:
                src = half.part2.at[block_at(k, mask), :]
            elif WIRE[s] == BF16:
                half.wire1[k * 4 + mask // 4] = half.acc2[k * 8 + mask // 2].astype(BF16)
                src = half.wire1.at[k * 4 + mask // 4]
            else:
                src = half.acc2.at[k * 8 + mask // 2]
            slot = k * 15 + mask - 1
            copy = remote(
                src, landing(k, s, mask ^ (1 << s)), half.rs_send.at[slot], half.rs_recv.at[slot],
                near[(k + s) % 4],
            )
            copy.start()
            copies[k, mask] = copy
            sends.append(copy)

        def urgency(mask):
            rest = mask & ~1
            return (first_step(rest) if rest else 4, -mask)

        for mask in sorted((m for m in range(16) if m & 1), key=urgency):
            for k in range(STREAMS):
                send(k, mask)
        n = 0
        entries = sorted((m for m in range(16) if not m & 1), key=lambda m: (first_step(m) if m else 4, -m))
        for mask in entries:
            steps = first_step(mask) if mask else 4
            for k in range(STREAMS):
                yield start + 2.5 + flow * n / 32
                n += 1
                value = half.part2[block_at(k, mask), :].astype(F32)
                for s in range(steps):
                    copies[k, mask | 1 << s].wait_recv()
                    value = value + landing(k, s, mask)[...].astype(F32)
                if mask:
                    half.acc2[k * 8 + mask // 2] = value
                    send(k, mask)
                else:
                    ns_ref[pl.ds(k * Q, Q), pl.ds(lane, H)] = value

    def prepare():
        yield 0.5
        for half in halves:
            half.acc[0] = jnp.zeros((TILE, H), F32)

    a, b = halves

    def first():
        yield from gather(a, 0.0, 8.0)
        yield from multiply(a, True, a.gathered, a.part, 10.5, 0.35)
        yield from exchange(a, 17.5, 17.5, 14.8, 7.4)
        yield from multiply(a, False, a.columns, a.part2, 46.0, 0.35)
        yield from reduce(a, 0, 53.0, 12.0)

    def second():
        yield 7.0
        yield from gather(b, 7.0, 8.0)
        yield from multiply(b, True, b.gathered, b.part, 18.0, 0.35)
        yield from exchange(b, 25.0, 34.0, 20.0, 9.0)
        yield from multiply(b, False, b.columns, b.part2, 69.0, 0.35)
        yield from reduce(b, H, 76.0, 12.0)

    interleave([first(), prepare(), second()])

    rows = ns_ref[...]
    shared.gram_part[...] = lax.dot_general(
        rows, rows, (((0,), (0,)), ((), ())), precision=HI, preferred_element_type=F32
    )
    mine = rows_at(row * 0 + me * 16 + core * 8, 8, 8)
    copies = []
    for n, (r, p) in enumerate(everyone):
        theirs = rows_at(p * 16 + lax.rem(r, 2) * 8, 8, 8)
        copy = remote(
            shared.gram_part.at[theirs, :], shared.slabs.at[n], shared.slab_send.at[n], shared.slab_recv.at[n], (r, p)
        )
        copy.start()
        copies.append(copy)
    sends += copies
    total = shared.gram_part[mine, :]
    for n, copy in enumerate(copies):
        copy.wait_recv()
        total = total + shared.slabs[n]
    shared.slab[...] = total
    copies = []
    for d, device in enumerate(column):
        copy = remote(shared.slab, shared.z_in.at[z], shared.z_send.at[d], shared.z_recv.at[d], device)
        copy.start()
        copies.append(copy)
    sends += copies
    shared.z_in[z] = total
    for copy in copies:
        copy.wait_recv()
    total = shared.z_in[0]
    for d in range(1, 8):
        total = total + shared.z_in[d]
    gram_ref[mine, :] = total * (1.0 / ROWS)
    copies = []
    for n, device in enumerate(everyone):
        copy = remote(gram_ref.at[mine, :], gram_ref.at[mine, :], shared.out_send.at[n], shared.out_recv.at[n], device)
        copy.start()
        copies.append(copy)
    for copy in copies:
        copy.wait_recv()
    for copy in sends + copies:
        copy.wait_send()


PLAN = 2 * CAP + BR


def plan_kernel(rows_ref, cols_ref, count_ref, plan_ref):
    count = count_ref[0]
    for base, source, target in ((0, rows_ref, cols_ref), (PLAN, cols_ref, rows_ref)):
        to = [target[t] for t in range(CAP)]
        for s in range(CAP):
            at = jnp.int32(0)
            for t in range(s):
                at = jnp.where(to[t] == to[s], t + 1, at)
            plan_ref[base + s] = source[s]
            plan_ref[base + CAP + s] = at
        for b in range(BR):
            at = jnp.int32(0)
            for t in range(CAP):
                at = jnp.where((to[t] == b) & (t < count), t + 1, at)
            plan_ref[base + 2 * CAP + b] = at


def make_plan(rows, cols, count):
    smem = pl.BlockSpec(memory_space=pltpu.SMEM)
    return pl.pallas_call(
        plan_kernel,
        out_shape=jax.ShapeDtypeStruct((2 * PLAN,), jnp.int32),
        in_specs=[smem] * 3,
        out_specs=smem,
        name="plan",
    )(rows, cols, count)


def iterate_call(plan, tiles, sketch):
    smem = pl.BlockSpec(memory_space=pltpu.SMEM)
    scratch = [make() for _ in range(2) for make in HALF_SCRATCH.values()]
    scratch += [make() for make in SHARED_SCRATCH.values()]
    return pl.pallas_call(
        iterate,
        out_shape=(
            jax.ShapeDtypeStruct((SHARD, K), F32),
            jax.ShapeDtypeStruct((K, K), F32),
        ),
        in_specs=[smem, pl.BlockSpec(memory_space=pl.ANY), whole()],
        out_specs=(whole(), whole()),
        scratch_shapes=scratch,
        compiler_params=pltpu.CompilerParams(
            collective_id=0, has_side_effects=True, vmem_limit_bytes=VMEM_LIMIT
        ),
        name="iterate",
    )(plan, tiles, sketch)


OUTER = 64


def factor_kernel(gram_ref, ns_ref, basis_ref, factor_ref, work):
    i0 = lax.broadcasted_iota(jnp.int32, (K, K), 0)
    i1 = lax.broadcasted_iota(jnp.int32, (K, K), 1)
    work[:, :K] = gram_ref[...]
    work[:, K:] = (i0 == i1).astype(F32)
    sub = lax.broadcasted_iota(jnp.int32, (8, 128), 0)
    for o in range(K // OUTER):
        base = o * OUTER
        for p in range(OUTER // 8):
            j = base + p * 8
            panel = work[pl.ds(j, 8), :]
            if p:
                done = work[pl.ds(base, p * 8), :]
                panel = panel - lax.dot_general(
                    done[:, j : j + 8], done, (((0,), (0,)), ((), ())),
                    precision=HI, preferred_element_type=F32,
                )
            parts = [panel[:, q * 128 : (q + 1) * 128] for q in range(4)]
            cols = [jnp.broadcast_to(panel[:, j + k : j + k + 1], (8, 128)) for k in range(8)]
            for i in range(8):
                scale = lax.rsqrt(jnp.broadcast_to(cols[i][i : i + 1, :], (8, 128)))
                down = jnp.where(sub > i, cols[i] * scale, 0.0)
                for k in range(i + 1, 8):
                    cols[k] = cols[k] - down * (jnp.broadcast_to(cols[k][i : i + 1, :], (8, 128)) * scale)
                for q in range(4):
                    line = jnp.broadcast_to(parts[q][i : i + 1, :], (8, 128)) * scale
                    parts[q] = jnp.where(sub == i, line, parts[q] - down * line)
            for q in range(4):
                work[pl.ds(j, 8), q * 128 : (q + 1) * 128] = parts[q]
        rest = K - base - OUTER
        if rest:
            done = work[pl.ds(base, OUTER), :]
            work[pl.ds(base + OUTER, rest), :] = work[pl.ds(base + OUTER, rest), :] - lax.dot_general(
                done[:, base + OUTER : K], done, (((0,), (0,)), ((), ())),
                precision=HI, preferred_element_type=F32,
            )
    factor_ref[...] = jnp.where(i1 >= i0, work[:, :K], 0.0)
    inverse_t = jnp.where(i0 >= i1, work[:, K:], 0.0)
    basis_ref[...] = lax.dot_general(
        ns_ref[...], inverse_t, (((1,), (1,)), ((), ())), precision=HI, preferred_element_type=F32
    )


def factor_and_basis(gram, ns):
    return pl.pallas_call(
        factor_kernel,
        out_shape=(
            jax.ShapeDtypeStruct((SHARD, K), F32),
            jax.ShapeDtypeStruct((K, K), F32),
        ),
        in_specs=[whole(), whole()],
        out_specs=(whole(), whole()),
        scratch_shapes=[vmem((K, 2 * K), F32)],
        compiler_params=pltpu.CompilerParams(vmem_limit_bytes=VMEM_LIMIT),
        name="factor",
    )(gram, ns)


def body(tiles, tile_rows, tile_cols, tile_counts, sketch):
    plan = make_plan(tile_rows[0, 0], tile_cols[0, 0], tile_counts[0])
    ns, gram = iterate_call(plan, tiles[0, 0], sketch)
    return factor_and_basis(gram, ns)


def solution(mesh):
    return jax.shard_map(
        body,
        mesh=mesh,
        in_specs=(
            P("row", "col", None, None, None),
            P("row", "col", None),
            P("row", "col", None),
            P("row", "col"),
            P(("row", "col"), None),
        ),
        out_specs=(P(("row", "col"), None), P()),
        check_vma=False,
    )
```

time: 781 us -> 165 us (0.21)
  waiting for transfers between devices: 630 us -> 0 us
  Pallas kernels: 0 us -> 163 us
  other arithmetic: 57.4 us -> 0 us
  matrix products: 29.5 us -> 0 us
  local copies, waits for them, and re-layouts: 24.7 us -> 0 us
  loops' own time: 21.7 us -> 0 us
  between operations: 15.3 us -> 1.29 us
    reduce_scatter x2 -> x0, waiting for transfers between devices: 270 us -> none  [the longest x1 144 us: body(): lax.psum_scatter(partial_rows, 'col', scatter_dimension=0, tiled=True)]
    psum x1 -> x0, waiting for transfers between devices: 257 us -> none  [body(): gram_matrix = lax.psum(local_gram, ('row', 'col')) / total_rows]
    pallas_call x0 -> x3, Pallas kernels: none -> 163 us  [the longest x1 144 us: iterate_call(): pl.pallas_call(iterate, out_shape=(jax.ShapeDtypeStruct((SHARD, K), F32),...]
    all_gather x2 -> x0, waiting for transfers between devices: 102 us -> none  [the longest x1 58.4 us: body(): gathered = lax.all_gather(sketch, 'col', axis=0, tiled=True)]
    another operation x9 -> x0, other arithmetic: 53.7 us -> none  [the longest x6 34 us: body(): cholesky_lower = jnp.linalg.cholesky(gram_matrix)]
    dot_general x11 -> x0, matrix products: 26.8 us -> none  [the longest x5 12.2 us: transposed_step(): lax.dot_general(matrix, sketch_block, (((0,), (0,)), ((), ())), preferred...]
    another operation x3 -> x0, loops' own time: 21.7 us -> none  [the longest x1 11 us: body(): lax.fori_loop(0, live_count, transposed_step, jnp.zeros((BC * tile_size,...]
    dynamic_slice x20 -> x0, local copies, waits for them, and re-layouts: 12.5 us -> none  [the longest x5 3.32 us: transposed_step(): target = col_ids[slot_index] * tile_size]
  transfers between devices with their start and end apart: 5 -> 0, of which waited for: 5 -> 0; matrix products, arithmetic and copies ran while one was open for 0% -> 0% of each run, Pallas kernels for 0% -> 0%
where the time goes in v2:
time: 165 us
  Pallas kernels  163 us (99%)
    pallas_call x1, Pallas kernels, iterate_call(): pl.pallas_call(iterate, out_shape=(jax.ShapeDtypeStruct((SHARD, K), F32),...  144 us
    pallas_call x1, Pallas kernels, factor_and_basis(): pl.pallas_call(factor_kernel, out_shape=(jax.ShapeDtypeStruct((SHARD, K),...  17.4 us

profile of v2, /device:TPU:1, one launch (start us, length us, event | category | flops | bytes accessed | tf_op | source)
XLA Modules:
  0.0 164.7 jit_solution(5273353811391890566)
XLA Ops:
  1.3 1.8 %plan.1.plan_ref = s32[88]{0:T(128)} custom-call(s32[16]{0:T(128)} %bitcast.6, s32[16]{0:T(128)} %bitcast.7, s32[1]{0:T(128)} %bitcast.4.count_ref), custom_call_target="tpu_custom_call" | custom-call | tf_op jit(solution)/shard_map/plan/pallas_call | solution.py:491
  3.1 144.2 %iterate.1 = (f32[384,256]{1,0:T(8,128)}, f32[256,256]{1,0:T(8,128)}) custom-call(s32[88]{0:T(128)} %plan.1.plan_ref, bf16[16,512,512]{2,1,0:T(8,128)(2,1)} %bitcast.5, bf16[384,256]{1,0:T(8,128)(2,1)} %sketch_ref.1), custom_call_target="tpu_custom_call" | custom-call | tf_op jit(solution)/shard_map/iterate/pallas_call | solution.py:504
  147.3 17.4 %factor.1 = (f32[384,256]{1,0:T(8,128)}, f32[256,256]{1,0:T(8,128)}) custom-call(f32[256,256]{1,0:T(8,128)} %get-tuple-element.4.gram_ref, f32[384,256]{1,0:T(8,128)} %get-tuple-element.5.ns_ref), custom_call_target="tpu_custom_call" | custom-call | tf_op jit(solution)/shard_map/factor/pallas_call | solution.py:567

commit v3 on v2

v3 whole, which is shorter than its diff:
```python
import functools
import heapq

import jax
import jax.numpy as jnp
from jax import lax
from jax.experimental import pallas as pl
from jax.experimental.pallas import tpu as pltpu
from jax.sharding import PartitionSpec as P

TILE = 512
K = 256
H = 128
BR = 12
BC = 12
CAP = 16
SHARD = 384
FULL = 6144
UNIT = 32
TU = TILE // UNIT
PU = 96 // UNIT
ROWS = 98304
STREAMS = 4
Q = SHARD // STREAMS
MESH = pl.DeviceIdType.MESH
HI = lax.Precision.HIGHEST
VMEM_LIMIT = 60 * 1024 * 1024
F32 = jnp.float32
BF16 = jnp.bfloat16
PARTS = 4
PART = SHARD // PARTS
CHAINS = tuple((1 - 2 * (p % 2), p, 4) for p in range(PARTS)) + tuple((2 * (p % 2) - 1, p, 3) for p in range(PARTS))
WIRE = (BF16, BF16, F32, F32)


def vmem(shape, dtype):
    return pltpu.VMEM(shape, dtype)


def dma(n):
    return pltpu.SemaphoreType.DMA((n,))


def whole():
    return pl.BlockSpec(memory_space=pltpu.VMEM)


def flip(i, g):
    x, y = lax.rem(i, 4), lax.div(i, 4)
    if g == 0:
        return i + 1 - 2 * lax.rem(x, 2)
    if g == 1:
        return i + 3 - 2 * x
    if g == 2:
        return i + 4 - 8 * lax.rem(y, 2)
    return i + 12 - 8 * y


def rows_at(start, size, step):
    return pl.ds(pl.multiple_of(start, step), size)


def remote(src, dst, send_sem, recv_sem, device):
    return pltpu.make_async_remote_copy(
        src_ref=src,
        dst_ref=dst,
        send_sem=send_sem,
        recv_sem=recv_sem,
        device_id=device,
        device_id_type=MESH,
    )


def last_step(mask):
    return mask.bit_length() - 1


def first_step(mask):
    return (mask & -mask).bit_length() - 1


def interleave(processes):
    queue = []
    for n, process in enumerate(processes):
        heapq.heappush(queue, (next(process), n, process))
    while queue:
        _, n, process = heapq.heappop(queue)
        try:
            heapq.heappush(queue, (next(process), n, process))
        except StopIteration:
            pass


def wide(x):
    return jnp.broadcast_to(x, (8, H))


def matmul(a, b, contract):
    return lax.dot_general(a, b, (contract, ((), ())), precision=HI, preferred_element_type=F32)


def eliminate(work):
    sub = lax.broadcasted_iota(jnp.int32, (8, H), 0)
    panels = H // 8
    below = None
    for p in range(panels):
        j = p * 8
        parts = [work[pl.ds(j, 8), :H], work[pl.ds(j, 8), H:]] if below is None else below
        cols = [wide(parts[0][:, j + k : j + k + 1]) for k in range(8)]
        below = None
        if p + 1 < panels:
            m = j + 8
            rows = work[pl.ds(m, 8), :]
            if p:
                done = work[pl.ds(0, j), :]
                rows = rows - matmul(done[:, m : m + 8], done, ((0,), (0,)))
            below = [rows[:, :H], rows[:, H:]]
            under = [wide(below[0][:, j + k : j + k + 1]) for k in range(8)]
        for i in range(8):
            scale = lax.rsqrt(wide(cols[i][i : i + 1, :]))
            down = jnp.where(sub > i, cols[i] * scale, 0.0)
            if below is not None:
                drop = under[i] * scale
            for k in range(i + 1, 8):
                line = wide(cols[k][i : i + 1, :]) * scale
                cols[k] = cols[k] - down * line
                if below is not None:
                    under[k] = under[k] - drop * line
            for q in range(2):
                line = wide(parts[q][i : i + 1, :]) * scale
                parts[q] = jnp.where(sub == i, line, parts[q] - down * line)
                if below is not None:
                    below[q] = below[q] - drop * line
        for q in range(2):
            work[pl.ds(j, 8), q * H : (q + 1) * H] = parts[q]
        yield


HALF_SCRATCH = dict(
    shard=lambda: vmem((SHARD // UNIT, UNIT, H), BF16),
    gathered=lambda: vmem((FULL // UNIT, UNIT, H), BF16),
    ag_send=lambda: dma(STREAMS * 15),
    ag_recv=lambda: dma(STREAMS * 15),
    acc=lambda: vmem((CAP + 1, TILE, H), F32),
    part=lambda: vmem((FULL, H), F32),
    pair_buf=lambda: vmem((8 * PARTS, PART, H), F32),
    sums=lambda: vmem((8 * PARTS, PART, H), F32),
    landed=lambda: vmem((8 * PARTS, PART, H), F32),
    pair_send=lambda: dma(8 * PARTS),
    pair_recv=lambda: dma(8 * PARTS),
    chain_send=lambda: dma(8 * PARTS),
    chain_recv=lambda: dma(8 * PARTS),
    own=lambda: vmem((SHARD // UNIT, UNIT, H), BF16),
    columns=lambda: vmem((FULL // UNIT, UNIT, H), BF16),
    gather_send=lambda: dma(8 * PARTS),
    gather_recv=lambda: dma(8 * PARTS),
    twin_send=lambda: dma(9 * PARTS),
    twin_recv=lambda: dma(9 * PARTS),
    part2=lambda: vmem((FULL, H), BF16),
    land0=lambda: vmem((STREAMS * 8, Q, H), BF16),
    land1=lambda: vmem((STREAMS * 4, Q, H), WIRE[1]),
    land2=lambda: vmem((STREAMS * 3, Q, H), F32),
    acc2=lambda: vmem((STREAMS * 8, Q, H), F32),
    wire1=lambda: vmem((STREAMS * 4, Q, H), BF16),
    rs_send=lambda: dma(STREAMS * 15),
    rs_recv=lambda: dma(STREAMS * 15),
)

SHARED_SCRATCH = dict(
    tiles=lambda: vmem((CAP, TILE, TILE), BF16),
    tile_sem=lambda: dma(CAP),
    work=lambda: vmem((H, 2 * H), F32),
    early_part=lambda: vmem((H, H), F32),
    early_in=lambda: vmem((16, 8, H), F32),
    early_row=lambda: vmem((16, 8, H), F32),
    early_slab=lambda: vmem((8, H), F32),
    early_sum=lambda: vmem((8, H), F32),
    early_gram=lambda: vmem((H, H), F32),
    early_send=lambda: dma(45),
    early_recv=lambda: dma(45),
    late_part=lambda: vmem((K, H), F32),
    slabs=lambda: vmem((31, 8, H), F32),
    slab=lambda: vmem((8, H), F32),
    slab_send=lambda: dma(31),
    slab_recv=lambda: dma(31),
    z_in=lambda: vmem((8, 8, H), F32),
    z_send=lambda: dma(7),
    z_recv=lambda: dma(7),
    out_send=lambda: dma(31),
    out_recv=lambda: dma(31),
)


class Refs:
    pass


def named(names, refs):
    out = Refs()
    for name, ref in zip(names, refs):
        setattr(out, name, ref)
    return out


def iterate(rows_ref, cols_ref, count_ref, tiles_ref, sketch_ref, ns_ref, early_ref, late_ref, *scratch):
    nh = len(HALF_SCRATCH)
    halves = [named(HALF_SCRATCH, scratch[i * nh : (i + 1) * nh]) for i in (0, 1)]
    shared = named(SHARED_SCRATCH, scratch[2 * nh :])

    row, me = lax.axis_index("row"), lax.axis_index("col")
    z, core = lax.div(row, 2), lax.rem(row, 2)
    other = row + 1 - 2 * core
    twin = (other, me)
    near = [(row, flip(me, g)) for g in range(4)]
    plane = [lax.rem(me + d, 16) for d in range(1, 16)]

    def ring(d):
        return lax.rem(z + d + 8, 8)

    side = {1: (2 * ring(1) + core, me), -1: (2 * ring(-1) + core, me)}
    column = [(2 * ring(d) + core, me) for d in range(1, 8)]
    everyone = [twin] + [(r, p) for p in plane for r in (row, other)]
    line = [(lax.rem(row + d, 16), me) for d in range(1, 16)]

    loads = []
    for s in range(CAP):
        load = pltpu.make_async_copy(tiles_ref.at[s], shared.tiles.at[s], shared.tile_sem.at[s])
        load.start()
        loads.append(load)
    for i, half in enumerate(halves):
        half.shard[...] = sketch_ref[:, i * H : (i + 1) * H].reshape(SHARD // UNIT, UNIT, H)

    barrier = pltpu.get_barrier_semaphore()
    greeted = everyone[1:] + line
    for device in greeted:
        pl.semaphore_signal(barrier, inc=1, device_id=device, device_id_type=MESH)
    pl.semaphore_wait(barrier, len(greeted))

    sends = []
    plan = {}

    def places(targets):
        to = [targets[t] for t in range(CAP)]
        count = count_ref[0]
        before, ends = [], []
        for s in range(CAP):
            at = jnp.int32(0)
            for t in range(s):
                at = jnp.where(to[t] == to[s], t + 1, at)
            before.append(at)
        for b in range(BR):
            at = jnp.int32(0)
            for t in range(CAP):
                at = jnp.where((to[t] == b) & (t < count), t + 1, at)
            ends.append(at)
        return before, ends

    def gather(half, start, flow):
        copies = {}
        half.gathered[pl.ds(me * (SHARD // UNIT), SHARD // UNIT)] = half.shard[...]

        def block_at(k, mask):
            block = me
            for s in range(4):
                if mask >> s & 1:
                    block = flip(block, (k + s) % 4)
            return pl.ds(block * (SHARD // UNIT) + k * (Q // UNIT), Q // UNIT)

        def forward(k, mask, s):
            at = block_at(k, mask)
            src = half.shard.at[pl.ds(k * (Q // UNIT), Q // UNIT)] if mask == 0 else half.gathered.at[at]
            slot = k * 15 + (mask | 1 << s) - 1
            copy = remote(
                src, half.gathered.at[at], half.ag_send.at[slot], half.ag_recv.at[slot], near[(k + s) % 4]
            )
            copy.start()
            copies[k, mask | 1 << s] = copy
            sends.append(copy)

        for s in range(4):
            for k in range(STREAMS):
                forward(k, 0, s)
        masks = sorted(range(1, 16), key=lambda m: (m.bit_count(), last_step(m), m))
        n = 0
        for mask in masks:
            for k in range(STREAMS):
                yield start + 3 + flow * n / 60
                n += 1
                copies[k, mask].wait_recv()
                for s in range(last_step(mask) + 1, 4):
                    forward(k, mask, s)

    def multiply(half, transposed, source, result, start, per_tile):
        src = rows_ref if transposed else cols_ref
        before, ends = plan[transposed]
        dims = (((0,), (0,)), ((), ())) if transposed else (((1,), (0,)), ((), ()))
        for s in range(CAP):
            yield start + per_tile * s
            if loads[s] is not None:
                loads[s].wait()
                loads[s] = None
            block = source[pl.ds(src[s] * TU, TU)].reshape(TILE, H)
            for u in range(2):
                part = pl.ds(u * 256, 256)
                tile = shared.tiles[s, :, part] if transposed else shared.tiles[s, part, :]
                half.acc[s + 1, part, :] = half.acc[before[s], part, :] + lax.dot_general(
                    tile, block, dims, preferred_element_type=F32
                )
        for b in range(BR):
            yield start + per_tile * CAP + 0.08 * b
            result[pl.ds(b * TILE, TILE), :] = half.acc[ends[b]].astype(result.dtype)

    def exchange(half, start, ring_start, reduce_flow, gather_flow):
        yield start
        order = []
        for t in range(1, 5):
            for direction, part, hops in CHAINS:
                if t <= hops:
                    item = (direction * (hops + 1 - t) % 8, part)
                    if item not in order:
                        order.append(item)
        order += [(0, part) for part in range(PARTS)]
        pair = {}
        for d, part in order:
            slot = d * PARTS + part
            theirs = rows_at((2 * ring(d) + 1 - core) * SHARD + part * PART, PART, PART)
            pair[d, part] = remote(
                half.part.at[theirs, :], half.pair_buf.at[slot],
                half.pair_send.at[slot], half.pair_recv.at[slot], twin,
            )
            pair[d, part].start()
            sends.append(pair[d, part])
        arrived = set()

        def chip_sum(d, part):
            d = d % 8
            slot = d * PARTS + part
            if (d, part) not in arrived:
                pair[d, part].wait_recv()
                arrived.add((d, part))
            mine = rows_at((2 * ring(d) + core) * SHARD + part * PART, PART, PART)
            return half.part[mine, :] + half.pair_buf[slot]

        last = {}
        n_sent = 0
        for t in range(1, 5):
            for n, (direction, part, hops) in enumerate(CHAINS):
                if t > hops:
                    continue
                yield ring_start + 2 + reduce_flow * n_sent / (7 * PARTS)
                n_sent += 1
                slot = n * 4 + t - 1
                value = chip_sum(direction * (hops + 1 - t), part)
                if t > 1:
                    last[n].wait_recv()
                    value = value + half.landed[slot - 1]
                half.sums[slot] = value
                copy = remote(
                    half.sums.at[slot], half.landed.at[slot],
                    half.chain_send.at[slot], half.chain_recv.at[slot], side[direction],
                )
                copy.start()
                last[n] = copy
                sends.append(copy)
        begin = ring_start + 3 + reduce_flow
        twins = []
        moving = {}

        def spread(src, at, slot):
            copy = remote(src, half.columns.at[at], half.twin_send.at[slot], half.twin_recv.at[slot], twin)
            copy.start()
            twins.append(copy)
            sends.append(copy)

        def pass_on(src, at, n, t):
            slot = n * 4 + t
            copy = remote(
                src, half.columns.at[at],
                half.gather_send.at[slot], half.gather_recv.at[slot], side[CHAINS[n][0]],
            )
            copy.start()
            moving[n] = copy
            sends.append(copy)

        for part in range(PARTS):
            yield begin + 0.1 * part
            value = chip_sum(0, part)
            for n in (part + PARTS, part):
                last[n].wait_recv()
                value = value + half.landed[n * 4 + CHAINS[n][2] - 1]
            local = pl.ds(part * PU, PU)
            rounded = value.astype(BF16).reshape(PU, UNIT, H)
            half.own[local] = rounded
            at = pl.ds((row * PARTS + part) * PU, PU)
            half.columns[at] = rounded
            for n in range(2 * PARTS):
                if CHAINS[n][1] == part:
                    pass_on(half.own.at[local], at, n, 0)
            spread(half.own.at[local], at, part)
        n_got = 0
        for t in range(1, 5):
            for n, (direction, part, hops) in enumerate(CHAINS):
                if t > hops:
                    continue
                yield begin + 2 + gather_flow * n_got / (7 * PARTS)
                n_got += 1
                moving[n].wait_recv()
                at = pl.ds(((2 * ring(-direction * t) + core) * PARTS + part) * PU, PU)
                if t < hops:
                    pass_on(half.columns.at[at], at, n, t)
                spread(half.columns.at[at], at, PARTS + n * 4 + t - 1)
        for copy in twins:
            yield begin + 3 + gather_flow
            copy.wait_recv()

    def reduce(half, lane, start, flow):
        yield start
        copies = {}

        def block_at(k, mask):
            block = me
            for s in range(4):
                if mask >> s & 1:
                    block = flip(block, (k + s) % 4)
            return rows_at(block * SHARD + k * Q, Q, 16)

        def landing(k, s, mask):
            if s == 0:
                return half.land0.at[k * 8 + mask // 2]
            if s == 1:
                return half.land1.at[k * 4 + mask // 4]
            return half.land2.at[k * 3 + (mask // 8 if s == 2 else 2)]

        def send(k, mask):
            s = first_step(mask)
            if s == 0:
                src = half.part2.at[block_at(k, mask), :]
            elif WIRE[s] == BF16:
                half.wire1[k * 4 + mask // 4] = half.acc2[k * 8 + mask // 2].astype(BF16)
                src = half.wire1.at[k * 4 + mask // 4]
            else:
                src = half.acc2.at[k * 8 + mask // 2]
            slot = k * 15 + mask - 1
            copy = remote(
                src, landing(k, s, mask ^ (1 << s)), half.rs_send.at[slot], half.rs_recv.at[slot],
                near[(k + s) % 4],
            )
            copy.start()
            copies[k, mask] = copy
            sends.append(copy)

        def urgency(mask):
            rest = mask & ~1
            return (first_step(rest) if rest else 4, -mask)

        for mask in sorted((m for m in range(16) if m & 1), key=urgency):
            for k in range(STREAMS):
                send(k, mask)
        n = 0
        entries = sorted((m for m in range(16) if not m & 1), key=lambda m: (first_step(m) if m else 4, -m))
        for mask in entries:
            steps = first_step(mask) if mask else 4
            for k in range(STREAMS):
                yield start + 2.5 + flow * n / 32
                n += 1
                value = half.part2[block_at(k, mask), :].astype(F32)
                for s in range(steps):
                    copies[k, mask | 1 << s].wait_recv()
                    value = value + landing(k, s, mask)[...].astype(F32)
                if mask:
                    half.acc2[k * 8 + mask // 2] = value
                    send(k, mask)
                else:
                    ns_ref[pl.ds(k * Q, Q), pl.ds(lane, H)] = value

    def prepare():
        yield 0.5
        for half in halves:
            half.acc[0] = jnp.zeros((TILE, H), F32)
        plan[True] = places(cols_ref)
        plan[False] = places(rows_ref)

    def early(start, plane_at, line_at, eliminate_at):
        yield start
        rows = ns_ref[:, :H]
        shared.early_part[...] = lax.dot_general(
            rows, rows, (((0,), (0,)), ((), ())), precision=HI, preferred_element_type=F32
        )
        mine = rows_at(me * 8, 8, 8)
        copies = []
        for d, p in enumerate(plane):
            copy = remote(
                shared.early_part.at[rows_at(p * 8, 8, 8), :], shared.early_in.at[d],
                shared.early_send.at[d], shared.early_recv.at[d], (row, p),
            )
            copy.start()
            copies.append(copy)
        sends.extend(copies)
        yield plane_at
        total = shared.early_part[mine, :]
        for d, copy in enumerate(copies):
            copy.wait_recv()
            total = total + shared.early_in[d]
        shared.early_slab[...] = total
        shared.early_row[row] = total
        copies = []
        for d, device in enumerate(line):
            copy = remote(
                shared.early_slab, shared.early_row.at[row],
                shared.early_send.at[15 + d], shared.early_recv.at[15 + d], device,
            )
            copy.start()
            copies.append(copy)
        sends.extend(copies)
        yield line_at
        for copy in copies:
            copy.wait_recv()
        total = shared.early_row[0]
        for d in range(1, 16):
            total = total + shared.early_row[d]
        total = total * (1.0 / ROWS)
        shared.early_sum[...] = total
        shared.early_gram[mine, :] = total
        copies = []
        for d, p in enumerate(plane):
            copy = remote(
                shared.early_sum, shared.early_gram.at[mine, :],
                shared.early_send.at[30 + d], shared.early_recv.at[30 + d], (row, p),
            )
            copy.start()
            copies.append(copy)
        sends.extend(copies)
        yield eliminate_at
        for copy in copies:
            copy.wait_recv()
        i0 = lax.broadcasted_iota(jnp.int32, (H, H), 0)
        i1 = lax.broadcasted_iota(jnp.int32, (H, H), 1)
        shared.work[:, :H] = shared.early_gram[...]
        shared.work[:, H:] = (i0 == i1).astype(F32)
        for n, _ in enumerate(eliminate(shared.work)):
            yield eliminate_at + 0.4 * n
        early_ref[:, :H] = jnp.where(i1 >= i0, shared.work[:, :H], 0.0)
        early_ref[:, H:] = jnp.where(i0 >= i1, shared.work[:, H:], 0.0)

    def late(start):
        yield start
        shared.late_part[...] = lax.dot_general(
            ns_ref[...], ns_ref[:, H:], (((0,), (0,)), ((), ())), precision=HI, preferred_element_type=F32
        )
        mine = rows_at(me * 16 + core * 8, 8, 8)
        copies = []
        for n, (r, p) in enumerate(everyone):
            theirs = rows_at(p * 16 + lax.rem(r, 2) * 8, 8, 8)
            copy = remote(
                shared.late_part.at[theirs, :], shared.slabs.at[n],
                shared.slab_send.at[n], shared.slab_recv.at[n], (r, p),
            )
            copy.start()
            copies.append(copy)
        sends.extend(copies)
        yield start + 5
        total = shared.late_part[mine, :]
        for n, copy in enumerate(copies):
            copy.wait_recv()
            total = total + shared.slabs[n]
        shared.slab[...] = total
        copies = []
        for d, device in enumerate(column):
            copy = remote(shared.slab, shared.z_in.at[z], shared.z_send.at[d], shared.z_recv.at[d], device)
            copy.start()
            copies.append(copy)
        sends.extend(copies)
        shared.z_in[z] = total
        yield start + 9
        for copy in copies:
            copy.wait_recv()
        total = shared.z_in[0]
        for d in range(1, 8):
            total = total + shared.z_in[d]
        late_ref[mine, :] = total * (1.0 / ROWS)
        copies = []
        for n, device in enumerate(everyone):
            copy = remote(
                late_ref.at[mine, :], late_ref.at[mine, :], shared.out_send.at[n], shared.out_recv.at[n], device
            )
            copy.start()
            copies.append(copy)
        sends.extend(copies)
        yield start + 14
        for copy in copies:
            copy.wait_recv()

    a, b = halves

    def first():
        yield from gather(a, 0.0, 12.5)
        yield from multiply(a, True, a.gathered, a.part, 16.0, 0.36)
        yield from exchange(a, 23.0, 23.0, 20.0, 12.0)
        yield from multiply(a, False, a.columns, a.part2, 62.0, 0.3)
        yield from reduce(a, 0, 68.0, 16.0)
        yield from early(87.0, 93.0, 98.0, 104.0)

    def second():
        yield 9.0
        yield from gather(b, 13.2, 10.0)
        yield from multiply(b, True, b.gathered, b.part, 27.0, 0.36)
        yield from exchange(b, 34.0, 34.0, 30.0, 11.0)
        yield from multiply(b, False, b.columns, b.part2, 82.0, 0.3)
        yield from reduce(b, H, 88.0, 10.0)
        yield from late(101.5)

    interleave([first(), prepare(), second()])
    for copy in sends:
        copy.wait_send()


def iterate_call(tiles, rows, cols, count, sketch):
    smem = pl.BlockSpec(memory_space=pltpu.SMEM)
    scratch = [make() for _ in range(2) for make in HALF_SCRATCH.values()]
    scratch += [make() for make in SHARED_SCRATCH.values()]
    return pl.pallas_call(
        iterate,
        out_shape=(
            jax.ShapeDtypeStruct((SHARD, K), F32),
            jax.ShapeDtypeStruct((H, K), F32),
            jax.ShapeDtypeStruct((K, H), F32),
        ),
        in_specs=[smem, smem, smem, pl.BlockSpec(memory_space=pl.ANY), whole()],
        out_specs=(whole(), whole(), whole()),
        scratch_shapes=scratch,
        compiler_params=pltpu.CompilerParams(
            collective_id=0, has_side_effects=True, vmem_limit_bytes=VMEM_LIMIT
        ),
        name="iterate",
    )(rows, cols, count, tiles, sketch)


def factor_kernel(early_ref, late_ref, ns_ref, basis_ref, factor_ref, work):
    inverse_t = early_ref[:, H:]
    across = matmul(inverse_t, late_ref[:H, :], ((1,), (0,)))
    i0 = lax.broadcasted_iota(jnp.int32, (H, H), 0)
    i1 = lax.broadcasted_iota(jnp.int32, (H, H), 1)
    work[:, :H] = late_ref[H:, :] - matmul(across, across, ((0,), (0,)))
    work[:, H:] = (i0 == i1).astype(F32)
    factor_ref[:H, :H] = early_ref[:, :H]
    factor_ref[:H, H:] = across
    factor_ref[H:, :H] = jnp.zeros((H, H), F32)
    left = matmul(ns_ref[:, :H], inverse_t, ((1,), (1,)))
    basis_ref[:, :H] = left
    rest = ns_ref[:, H:] - matmul(left, across, ((1,), (0,)))
    for _ in eliminate(work):
        pass
    factor_ref[H:, H:] = jnp.where(i1 >= i0, work[:, :H], 0.0)
    basis_ref[:, H:] = matmul(rest, jnp.where(i0 >= i1, work[:, H:], 0.0), ((1,), (1,)))


def factor_and_basis(early, late, ns):
    return pl.pallas_call(
        factor_kernel,
        out_shape=(
            jax.ShapeDtypeStruct((SHARD, K), F32),
            jax.ShapeDtypeStruct((K, K), F32),
        ),
        in_specs=[whole(), whole(), whole()],
        out_specs=(whole(), whole()),
        scratch_shapes=[vmem((H, 2 * H), F32)],
        compiler_params=pltpu.CompilerParams(vmem_limit_bytes=VMEM_LIMIT),
        name="factor",
    )(early, late, ns)


def body(tiles, tile_rows, tile_cols, tile_counts, sketch):
    ns, early, late = iterate_call(tiles[0, 0], tile_rows[0, 0], tile_cols[0, 0], tile_counts[0], sketch)
    return factor_and_basis(early, late, ns)


def solution(mesh):
    return jax.shard_map(
        body,
        mesh=mesh,
        in_specs=(
            P("row", "col", None, None, None),
            P("row", "col", None),
            P("row", "col", None),
            P("row", "col"),
            P(("row", "col"), None),
        ),
        out_specs=(P(("row", "col"), None), P()),
        check_vma=False,
    )
```

time: 165 us -> 152 us (0.921)
  Pallas kernels: 163 us -> 150 us
    pallas_call x1, Pallas kernels: 17.4 us -> 7.34 us  [factor_and_basis(): pl.pallas_call(factor_kernel, out_shape=(jax.ShapeDtypeStruct((SHARD, K),...]
    pallas_call x1 -> x0, Pallas kernels: 1.77 us -> none  [make_plan(): pl.pallas_call(plan_kernel, out_shape=jax.ShapeDtypeStruct((2 * PLAN,), j...]
where the time goes in v3:
time: 152 us; the launch traced here: 151 us
  Pallas kernels  150 us (99%)
    pallas_call x1, Pallas kernels, iterate_call(): pl.pallas_call(iterate, out_shape=(jax.ShapeDtypeStruct((SHARD, K), F32),...  143 us
    pallas_call x1, Pallas kernels, factor_and_basis(): pl.pallas_call(factor_kernel, out_shape=(jax.ShapeDtypeStruct((SHARD, K),...  7.34 us

profile of v3, /device:TPU:1, one launch (start us, length us, event | category | flops | bytes accessed | tf_op | source)
XLA Modules:
  0.0 151.4 jit_solution(14360411198020390914)
XLA Ops:
  1.3 142.8 %iterate.1 = (f32[384,256]{1,0:T(8,128)}, f32[128,256]{1,0:T(8,128)}, f32[256,128]{1,0:T(8,128)}) custom-call(s32[16]{0:T(128)} %bitcast.6, s32[16]{0:T(128)} %bitcast.7, s32[1]{0:T(128)} %bitcast.4.count_ref, bf16[16,512,512]{2,1,0:T(8,128)(2,1)} %bitcast.5, bf16[384,256]{1,0:T(8,128)(2,1)} %sketch_ref.1), custom_call_target="tpu_custom_call" | custom-call | tf_op jit(solution)/shard_map/iterate/pallas_call | solution.py:621
  144.0 7.3 %factor.1 = (f32[384,256]{1,0:T(8,128)}, f32[256,256]{1,0:T(8,128)}) custom-call(f32[128,256]{1,0:T(8,128)} %get-tuple-element.5.early_ref, f32[256,128]{1,0:T(8,128)} %get-tuple-element.6.late_ref, f32[384,256]{1,0:T(8,128)} %get-tuple-element.7.ns_ref), custom_call_target="tpu_custom_call" | custom-call | tf_op jit(solution)/shard_map/factor/pallas_call | solution.py:658

commit v4 on v3

--- a/solution.py
+++ b/solution.py
@@ -77,6 +77,10 @@
 
 def first_step(mask):
     return (mask & -mask).bit_length() - 1
+
+
+def slot_of(n, t):
+    return n * 4 + t - 1 if n < PARTS else PARTS * 4 + (n - PARTS) * 3 + t - 1
 
 
 def interleave(processes):
@@ -139,30 +143,30 @@
 HALF_SCRATCH = dict(
     shard=lambda: vmem((SHARD // UNIT, UNIT, H), BF16),
     gathered=lambda: vmem((FULL // UNIT, UNIT, H), BF16),
-    ag_send=lambda: dma(STREAMS * 15),
+    ag_send=lambda: dma(1),
     ag_recv=lambda: dma(STREAMS * 15),
     acc=lambda: vmem((CAP + 1, TILE, H), F32),
     part=lambda: vmem((FULL, H), F32),
     pair_buf=lambda: vmem((8 * PARTS, PART, H), F32),
-    sums=lambda: vmem((8 * PARTS, PART, H), F32),
-    landed=lambda: vmem((8 * PARTS, PART, H), F32),
-    pair_send=lambda: dma(8 * PARTS),
+    sums=lambda: vmem((7 * PARTS, PART, H), F32),
+    landed=lambda: vmem((7 * PARTS, PART, H), F32),
+    pair_send=lambda: dma(1),
     pair_recv=lambda: dma(8 * PARTS),
-    chain_send=lambda: dma(8 * PARTS),
-    chain_recv=lambda: dma(8 * PARTS),
+    chain_send=lambda: dma(1),
+    chain_recv=lambda: dma(7 * PARTS),
     own=lambda: vmem((SHARD // UNIT, UNIT, H), BF16),
     columns=lambda: vmem((FULL // UNIT, UNIT, H), BF16),
-    gather_send=lambda: dma(8 * PARTS),
-    gather_recv=lambda: dma(8 * PARTS),
-    twin_send=lambda: dma(9 * PARTS),
-    twin_recv=lambda: dma(9 * PARTS),
+    gather_send=lambda: dma(1),
+    gather_recv=lambda: dma(7 * PARTS),
+    twin_send=lambda: dma(1),
+    twin_recv=lambda: dma(1),
     part2=lambda: vmem((FULL, H), BF16),
     land0=lambda: vmem((STREAMS * 8, Q, H), BF16),
     land1=lambda: vmem((STREAMS * 4, Q, H), WIRE[1]),
     land2=lambda: vmem((STREAMS * 3, Q, H), F32),
     acc2=lambda: vmem((STREAMS * 8, Q, H), F32),
     wire1=lambda: vmem((STREAMS * 4, Q, H), BF16),
-    rs_send=lambda: dma(STREAMS * 15),
+    rs_send=lambda: dma(2),
     rs_recv=lambda: dma(STREAMS * 15),
 )
 
@@ -176,18 +180,18 @@
     early_slab=lambda: vmem((8, H), F32),
     early_sum=lambda: vmem((8, H), F32),
     early_gram=lambda: vmem((H, H), F32),
-    early_send=lambda: dma(45),
-    early_recv=lambda: dma(45),
+    early_send=lambda: dma(3),
+    early_recv=lambda: dma(3),
     late_part=lambda: vmem((K, H), F32),
     slabs=lambda: vmem((31, 8, H), F32),
     slab=lambda: vmem((8, H), F32),
-    slab_send=lambda: dma(31),
-    slab_recv=lambda: dma(31),
+    slab_send=lambda: dma(1),
+    slab_recv=lambda: dma(1),
     z_in=lambda: vmem((8, 8, H), F32),
-    z_send=lambda: dma(7),
-    z_recv=lambda: dma(7),
-    out_send=lambda: dma(31),
-    out_recv=lambda: dma(31),
+    z_send=lambda: dma(1),
+    z_recv=lambda: dma(1),
+    out_send=lambda: dma(1),
+    out_recv=lambda: dma(1),
 )
 
 
@@ -236,8 +240,13 @@
         pl.semaphore_signal(barrier, inc=1, device_id=device, device_id_type=MESH)
     pl.semaphore_wait(barrier, len(greeted))
 
-    sends = []
     plan = {}
+
+    def landed_all(view, sem):
+        remote(view, view, sem, sem, twin).wait_recv()
+
+    def left_all(view, sem):
+        remote(view, view, sem, sem, twin).wait_send()
 
     def places(targets):
         to = [targets[t] for t in range(CAP)]
@@ -271,11 +280,10 @@
             src = half.shard.at[pl.ds(k * (Q // UNIT), Q // UNIT)] if mask == 0 else half.gathered.at[at]
             slot = k * 15 + (mask | 1 << s) - 1
             copy = remote(
-                src, half.gathered.at[at], half.ag_send.at[slot], half.ag_recv.at[slot], near[(k + s) % 4]
+                src, half.gathered.at[at], half.ag_send.at[0], half.ag_recv.at[slot], near[(k + s) % 4]
             )
             copy.start()
             copies[k, mask | 1 << s] = copy
-            sends.append(copy)
 
         for s in range(4):
             for k in range(STREAMS):
@@ -326,10 +334,9 @@
             theirs = rows_at((2 * ring(d) + 1 - core) * SHARD + part * PART, PART, PART)
             pair[d, part] = remote(
                 half.part.at[theirs, :], half.pair_buf.at[slot],
-                half.pair_send.at[slot], half.pair_recv.at[slot], twin,
+                half.pair_send.at[0], half.pair_recv.at[slot], twin,
             )
             pair[d, part].start()
-            sends.append(pair[d, part])
         arrived = set()
 
         def chip_sum(d, part):
@@ -349,7 +356,7 @@
                     continue
                 yield ring_start + 2 + reduce_flow * n_sent / (7 * PARTS)
                 n_sent += 1
-                slot = n * 4 + t - 1
+                slot = slot_of(n, t)
                 value = chip_sum(direction * (hops + 1 - t), part)
                 if t > 1:
                     last[n].wait_recv()
@@ -357,37 +364,32 @@
                 half.sums[slot] = value
                 copy = remote(
                     half.sums.at[slot], half.landed.at[slot],
-                    half.chain_send.at[slot], half.chain_recv.at[slot], side[direction],
+                    half.chain_send.at[0], half.chain_recv.at[slot], side[direction],
                 )
                 copy.start()
                 last[n] = copy
-                sends.append(copy)
         begin = ring_start + 3 + reduce_flow
-        twins = []
         moving = {}
 
-        def spread(src, at, slot):
-            copy = remote(src, half.columns.at[at], half.twin_send.at[slot], half.twin_recv.at[slot], twin)
-            copy.start()
-            twins.append(copy)
-            sends.append(copy)
+        def spread(src, at):
+            copy = remote(src, half.columns.at[at], half.twin_send.at[0], half.twin_recv.at[0], twin)
+            copy.start()
 
         def pass_on(src, at, n, t):
-            slot = n * 4 + t
+            slot = slot_of(n, t + 1)
             copy = remote(
                 src, half.columns.at[at],
-                half.gather_send.at[slot], half.gather_recv.at[slot], side[CHAINS[n][0]],
+                half.gather_send.at[0], half.gather_recv.at[slot], side[CHAINS[n][0]],
             )
             copy.start()
             moving[n] = copy
-            sends.append(copy)
 
         for part in range(PARTS):
             yield begin + 0.1 * part
             value = chip_sum(0, part)
             for n in (part + PARTS, part):
                 last[n].wait_recv()
-                value = value + half.landed[n * 4 + CHAINS[n][2] - 1]
+                value = value + half.landed[slot_of(n, CHAINS[n][2])]
             local = pl.ds(part * PU, PU)
             rounded = value.astype(BF16).reshape(PU, UNIT, H)
             half.own[local] = rounded
@@ -396,7 +398,7 @@
             for n in range(2 * PARTS):
                 if CHAINS[n][1] == part:
                     pass_on(half.own.at[local], at, n, 0)
-            spread(half.own.at[local], at, part)
+            spread(half.own.at[local], at)
         n_got = 0
         for t in range(1, 5):
             for n, (direction, part, hops) in enumerate(CHAINS):
@@ -408,10 +410,9 @@
                 at = pl.ds(((2 * ring(-direction * t) + core) * PARTS + part) * PU, PU)
                 if t < hops:
                     pass_on(half.columns.at[at], at, n, t)
-                spread(half.columns.at[at], at, PARTS + n * 4 + t - 1)
-        for copy in twins:
-            yield begin + 3 + gather_flow
-            copy.wait_recv()
+                spread(half.columns.at[at], at)
+        yield begin + 3 + gather_flow
+        landed_all(half.columns.at[pl.ds(0, 8 * PARTS * PU)], half.twin_recv.at[0])
 
     def reduce(half, lane, start, flow):
         yield start
@@ -442,12 +443,11 @@
                 src = half.acc2.at[k * 8 + mask // 2]
             slot = k * 15 + mask - 1
             copy = remote(
-                src, landing(k, s, mask ^ (1 << s)), half.rs_send.at[slot], half.rs_recv.at[slot],
+                src, landing(k, s, mask ^ (1 << s)), half.rs_send.at[s // 2], half.rs_recv.at[slot],
                 near[(k + s) % 4],
             )
             copy.start()
             copies[k, mask] = copy
-            sends.append(copy)
 
         def urgency(mask):
             rest = mask & ~1
@@ -487,52 +487,41 @@
             rows, rows, (((0,), (0,)), ((), ())), precision=HI, preferred_element_type=F32
         )
         mine = rows_at(me * 8, 8, 8)
-        copies = []
         for d, p in enumerate(plane):
             copy = remote(
                 shared.early_part.at[rows_at(p * 8, 8, 8), :], shared.early_in.at[d],
-                shared.early_send.at[d], shared.early_recv.at[d], (row, p),
-            )
-            copy.start()
-            copies.append(copy)
-        sends.extend(copies)
+                shared.early_send.at[0], shared.early_recv.at[0], (row, p),
+            )
+            copy.start()
         yield plane_at
         total = shared.early_part[mine, :]
-        for d, copy in enumerate(copies):
-            copy.wait_recv()
+        landed_all(shared.early_in.at[pl.ds(0, 15)], shared.early_recv.at[0])
+        for d in range(15):
             total = total + shared.early_in[d]
         shared.early_slab[...] = total
         shared.early_row[row] = total
-        copies = []
         for d, device in enumerate(line):
             copy = remote(
                 shared.early_slab, shared.early_row.at[row],
-                shared.early_send.at[15 + d], shared.early_recv.at[15 + d], device,
-            )
-            copy.start()
-            copies.append(copy)
-        sends.extend(copies)
+                shared.early_send.at[1], shared.early_recv.at[1], device,
+            )
+            copy.start()
         yield line_at
-        for copy in copies:
-            copy.wait_recv()
+        landed_all(shared.early_in.at[pl.ds(0, 15)], shared.early_recv.at[1])
         total = shared.early_row[0]
         for d in range(1, 16):
             total = total + shared.early_row[d]
         total = total * (1.0 / ROWS)
         shared.early_sum[...] = total
         shared.early_gram[mine, :] = total
-        copies = []
         for d, p in enumerate(plane):
             copy = remote(
                 shared.early_sum, shared.early_gram.at[mine, :],
-                shared.early_send.at[30 + d], shared.early_recv.at[30 + d], (row, p),
-            )
-            copy.start()
-            copies.append(copy)
-        sends.extend(copies)
+                shared.early_send.at[2], shared.early_recv.at[2], (row, p),
+            )
+            copy.start()
         yield eliminate_at
-        for copy in copies:
-            copy.wait_recv()
+        landed_all(shared.early_in.at[pl.ds(0, 15)], shared.early_recv.at[2])
         i0 = lax.broadcasted_iota(jnp.int32, (H, H), 0)
         i1 = lax.broadcasted_iota(jnp.int32, (H, H), 1)
         shared.work[:, :H] = shared.early_gram[...]
@@ -548,47 +537,36 @@
             ns_ref[...], ns_ref[:, H:], (((0,), (0,)), ((), ())), precision=HI, preferred_element_type=F32
         )
         mine = rows_at(me * 16 + core * 8, 8, 8)
-        copies = []
         for n, (r, p) in enumerate(everyone):
             theirs = rows_at(p * 16 + lax.rem(r, 2) * 8, 8, 8)
             copy = remote(
                 shared.late_part.at[theirs, :], shared.slabs.at[n],
-                shared.slab_send.at[n], shared.slab_recv.at[n], (r, p),
-            )
-            copy.start()
-            copies.append(copy)
-        sends.extend(copies)
+                shared.slab_send.at[0], shared.slab_recv.at[0], (r, p),
+            )
+            copy.start()
         yield start + 5
         total = shared.late_part[mine, :]
-        for n, copy in enumerate(copies):
-            copy.wait_recv()
+        landed_all(shared.slabs, shared.slab_recv.at[0])
+        for n in range(31):
             total = total + shared.slabs[n]
         shared.slab[...] = total
-        copies = []
         for d, device in enumerate(column):
-            copy = remote(shared.slab, shared.z_in.at[z], shared.z_send.at[d], shared.z_recv.at[d], device)
-            copy.start()
-            copies.append(copy)
-        sends.extend(copies)
+            copy = remote(shared.slab, shared.z_in.at[z], shared.z_send.at[0], shared.z_recv.at[0], device)
+            copy.start()
         shared.z_in[z] = total
         yield start + 9
-        for copy in copies:
-            copy.wait_recv()
+        landed_all(shared.z_in.at[pl.ds(0, 7)], shared.z_recv.at[0])
         total = shared.z_in[0]
         for d in range(1, 8):
             total = total + shared.z_in[d]
         late_ref[mine, :] = total * (1.0 / ROWS)
-        copies = []
         for n, device in enumerate(everyone):
             copy = remote(
-                late_ref.at[mine, :], late_ref.at[mine, :], shared.out_send.at[n], shared.out_recv.at[n], device
-            )
-            copy.start()
-            copies.append(copy)
-        sends.extend(copies)
+                late_ref.at[mine, :], late_ref.at[mine, :], shared.out_send.at[0], shared.out_recv.at[0], device
+            )
+            copy.start()
         yield start + 14
-        for copy in copies:
-            copy.wait_recv()
+        landed_all(shared.slabs, shared.out_recv.at[0])
 
     a, b = halves
 
@@ -610,8 +588,19 @@
         yield from late(101.5)
 
     interleave([first(), prepare(), second()])
-    for copy in sends:
-        copy.wait_send()
+    for half in halves:
+        left_all(half.gathered.at[pl.ds(0, 15 * SHARD // UNIT)], half.ag_send.at[0])
+        left_all(half.pair_buf, half.pair_send.at[0])
+        left_all(half.sums, half.chain_send.at[0])
+        left_all(half.columns.at[pl.ds(0, 7 * PARTS * PU)], half.gather_send.at[0])
+        left_all(half.columns.at[pl.ds(0, 8 * PARTS * PU)], half.twin_send.at[0])
+        left_all(half.columns.at[pl.ds(0, 12 * STREAMS * PU)], half.rs_send.at[0])
+        left_all(half.acc2.at[pl.ds(0, 3 * STREAMS)], half.rs_send.at[1])
+    for n in range(3):
+        left_all(shared.early_in.at[pl.ds(0, 15)], shared.early_send.at[n])
+    left_all(shared.slabs, shared.slab_send.at[0])
+    left_all(shared.z_in.at[pl.ds(0, 7)], shared.z_send.at[0])
+    left_all(shared.slabs, shared.out_send.at[0])
 
 
 def iterate_call(tiles, rows, cols, count, sketch):

time: 152 us -> 143 us (0.941)
  Pallas kernels: 150 us -> 142 us
    pallas_call x1, Pallas kernels: 143 us -> 135 us  [iterate_call(): pl.pallas_call(iterate, out_shape=(jax.ShapeDtypeStruct((SHARD, K), F32),...]
where the time goes in v4:
time: 143 us
  Pallas kernels  142 us (99%)
    pallas_call x1, Pallas kernels, iterate_call(): pl.pallas_call(iterate, out_shape=(jax.ShapeDtypeStruct((SHARD, K), F32),...  135 us
    pallas_call x1, Pallas kernels, factor_and_basis(): pl.pallas_call(factor_kernel, out_shape=(jax.ShapeDtypeStruct((SHARD, K),...  7.34 us

profile of v4, /device:TPU:1, one launch (start us, length us, event | category | flops | bytes accessed | tf_op | source)
XLA Modules:
  0.0 143.3 jit_solution(2235125790606112813)
XLA Ops:
  1.3 134.7 %iterate.1 = (f32[384,256]{1,0:T(8,128)}, f32[128,256]{1,0:T(8,128)}, f32[256,128]{1,0:T(8,128)}) custom-call(s32[16]{0:T(128)} %bitcast.6, s32[16]{0:T(128)} %bitcast.7, s32[1]{0:T(128)} %bitcast.4.count_ref, bf16[16,512,512]{2,1,0:T(8,128)(2,1)} %bitcast.5, bf16[384,256]{1,0:T(8,128)(2,1)} %sketch_ref.1), custom_call_target="tpu_custom_call" | custom-call | tf_op jit(solution)/shard_map/iterate/pallas_call | solution.py:610
  136.0 7.3 %factor.1 = (f32[384,256]{1,0:T(8,128)}, f32[256,256]{1,0:T(8,128)}) custom-call(f32[128,256]{1,0:T(8,128)} %get-tuple-element.5.early_ref, f32[256,128]{1,0:T(8,128)} %get-tuple-element.6.late_ref, f32[384,256]{1,0:T(8,128)} %get-tuple-element.7.ns_ref), custom_call_target="tpu_custom_call" | custom-call | tf_op jit(solution)/shard_map/factor/pallas_call | solution.py:647

commit v5 on v4

--- a/solution.py
+++ b/solution.py
@@ -318,7 +318,7 @@
             yield start + per_tile * CAP + 0.08 * b
             result[pl.ds(b * TILE, TILE), :] = half.acc[ends[b]].astype(result.dtype)
 
-    def exchange(half, start, ring_start, reduce_flow, gather_flow):
+    def exchange(half, start, reduce_at, own_at, gather_at, twins_at):
         yield start
         order = []
         for t in range(1, 5):
@@ -349,13 +349,11 @@
             return half.part[mine, :] + half.pair_buf[slot]
 
         last = {}
-        n_sent = 0
         for t in range(1, 5):
             for n, (direction, part, hops) in enumerate(CHAINS):
                 if t > hops:
                     continue
-                yield ring_start + 2 + reduce_flow * n_sent / (7 * PARTS)
-                n_sent += 1
+                yield reduce_at[t - 1] + 0.3 * n
                 slot = slot_of(n, t)
                 value = chip_sum(direction * (hops + 1 - t), part)
                 if t > 1:
@@ -368,7 +366,6 @@
                 )
                 copy.start()
                 last[n] = copy
-        begin = ring_start + 3 + reduce_flow
         moving = {}
 
         def spread(src, at):
@@ -385,7 +382,7 @@
             moving[n] = copy
 
         for part in range(PARTS):
-            yield begin + 0.1 * part
+            yield own_at + 0.02 * part
             value = chip_sum(0, part)
             for n in (part + PARTS, part):
                 last[n].wait_recv()
@@ -399,22 +396,20 @@
                 if CHAINS[n][1] == part:
                     pass_on(half.own.at[local], at, n, 0)
             spread(half.own.at[local], at)
-        n_got = 0
         for t in range(1, 5):
             for n, (direction, part, hops) in enumerate(CHAINS):
                 if t > hops:
                     continue
-                yield begin + 2 + gather_flow * n_got / (7 * PARTS)
-                n_got += 1
+                yield gather_at[t - 1] + 0.3 * n
                 moving[n].wait_recv()
                 at = pl.ds(((2 * ring(-direction * t) + core) * PARTS + part) * PU, PU)
                 if t < hops:
                     pass_on(half.columns.at[at], at, n, t)
                 spread(half.columns.at[at], at)
-        yield begin + 3 + gather_flow
+        yield twins_at
         landed_all(half.columns.at[pl.ds(0, 8 * PARTS * PU)], half.twin_recv.at[0])
 
-    def reduce(half, lane, start, flow):
+    def reduce(half, lane, start, at, flow):
         yield start
         copies = {}
 
@@ -456,13 +451,12 @@
         for mask in sorted((m for m in range(16) if m & 1), key=urgency):
             for k in range(STREAMS):
                 send(k, mask)
-        n = 0
         entries = sorted((m for m in range(16) if not m & 1), key=lambda m: (first_step(m) if m else 4, -m))
         for mask in entries:
             steps = first_step(mask) if mask else 4
             for k in range(STREAMS):
-                yield start + 2.5 + flow * n / 32
-                n += 1
+                at[steps - 1] += flow
+                yield at[steps - 1]
                 value = half.part2[block_at(k, mask), :].astype(F32)
                 for s in range(steps):
                     copies[k, mask | 1 << s].wait_recv()
@@ -527,7 +521,7 @@
         shared.work[:, :H] = shared.early_gram[...]
         shared.work[:, H:] = (i0 == i1).astype(F32)
         for n, _ in enumerate(eliminate(shared.work)):
-            yield eliminate_at + 0.4 * n
+            yield eliminate_at + (0 if n < 12 else 4.2)
         early_ref[:, :H] = jnp.where(i1 >= i0, shared.work[:, :H], 0.0)
         early_ref[:, H:] = jnp.where(i0 >= i1, shared.work[:, H:], 0.0)
 
@@ -573,19 +567,19 @@
     def first():
         yield from gather(a, 0.0, 12.5)
         yield from multiply(a, True, a.gathered, a.part, 16.0, 0.36)
-        yield from exchange(a, 23.0, 23.0, 20.0, 12.0)
+        yield from exchange(a, 23.0, (23.5, 29.0, 34.6, 40.0), 46.0, (49.0, 52.0, 55.5, 59.0), 61.4)
         yield from multiply(a, False, a.columns, a.part2, 62.0, 0.3)
-        yield from reduce(a, 0, 68.0, 16.0)
-        yield from early(87.0, 93.0, 98.0, 104.0)
+        yield from reduce(a, 0, 68.0, [70.5, 79.2, 82.4, 87.5], 0.1)
+        yield from early(88.2, 93.4, 97.6, 102.7)
 
     def second():
         yield 9.0
         yield from gather(b, 13.2, 10.0)
         yield from multiply(b, True, b.gathered, b.part, 27.0, 0.36)
-        yield from exchange(b, 34.0, 34.0, 30.0, 11.0)
-        yield from multiply(b, False, b.columns, b.part2, 82.0, 0.3)
-        yield from reduce(b, H, 88.0, 10.0)
-        yield from late(101.5)
+        yield from exchange(b, 34.0, (34.2, 42.6, 50.2, 57.0), 61.6, (64.5, 67.8, 71.2, 74.6), 77.4)
+        yield from multiply(b, False, b.columns, b.part2, 78.0, 0.3)
+        yield from reduce(b, H, 84.0, [87.0, 90.5, 93.5, 95.5], 0.2)
+        yield from late(97.5)
 
     interleave([first(), prepare(), second()])
     for half in halves:

time: 143 us -> 142 us (level)
  Pallas kernels: 142 us -> 140 us
    pallas_call x1, Pallas kernels: 135 us -> 133 us  [iterate_call(): pl.pallas_call(iterate, out_shape=(jax.ShapeDtypeStruct((SHARD, K), F32),...]
where the time goes in v5:
time: 142 us
  Pallas kernels  140 us (99%)
    pallas_call x1, Pallas kernels, iterate_call(): pl.pallas_call(iterate, out_shape=(jax.ShapeDtypeStruct((SHARD, K), F32),...  133 us
    pallas_call x1, Pallas kernels, factor_and_basis(): pl.pallas_call(factor_kernel, out_shape=(jax.ShapeDtypeStruct((SHARD, K),...  7.34 us

profile of v5, /device:TPU:1, one launch (start us, length us, event | category | flops | bytes accessed | tf_op | source)
XLA Modules:
  0.0 141.6 jit_solution(12888070058463357513)
XLA Ops:
  1.3 133.0 %iterate.1 = (f32[384,256]{1,0:T(8,128)}, f32[128,256]{1,0:T(8,128)}, f32[256,128]{1,0:T(8,128)}) custom-call(s32[16]{0:T(128)} %bitcast.6, s32[16]{0:T(128)} %bitcast.7, s32[1]{0:T(128)} %bitcast.4.count_ref, bf16[16,512,512]{2,1,0:T(8,128)(2,1)} %bitcast.5, bf16[384,256]{1,0:T(8,128)(2,1)} %sketch_ref.1), custom_call_target="tpu_custom_call" | custom-call | tf_op jit(solution)/shard_map/iterate/pallas_call | solution.py:604
  134.3 7.3 %factor.1 = (f32[384,256]{1,0:T(8,128)}, f32[256,256]{1,0:T(8,128)}) custom-call(f32[128,256]{1,0:T(8,128)} %get-tuple-element.5.early_ref, f32[256,128]{1,0:T(8,128)} %get-tuple-element.6.late_ref, f32[384,256]{1,0:T(8,128)} %get-tuple-element.7.ns_ref), custom_call_target="tpu_custom_call" | custom-call | tf_op jit(solution)/shard_map/factor/pallas_call | solution.py:641

commit v6 on v5

--- a/solution.py
+++ b/solution.py
@@ -264,7 +264,7 @@
             ends.append(at)
         return before, ends
 
-    def gather(half, start, flow):
+    def gather(half, start, flow, merged=False):
         copies = {}
         half.gathered[pl.ds(me * (SHARD // UNIT), SHARD // UNIT)] = half.shard[...]
 
@@ -280,7 +280,8 @@
             src = half.shard.at[pl.ds(k * (Q // UNIT), Q // UNIT)] if mask == 0 else half.gathered.at[at]
             slot = k * 15 + (mask | 1 << s) - 1
             copy = remote(
-                src, half.gathered.at[at], half.ag_send.at[0], half.ag_recv.at[slot], near[(k + s) % 4]
+                src, half.gathered.at[at], half.ag_send.at[0],
+                half.ag_recv.at[slot % 15 if merged else slot], near[(k + s) % 4]
             )
             copy.start()
             copies[k, mask | 1 << s] = copy
@@ -294,7 +295,10 @@
             for k in range(STREAMS):
                 yield start + 3 + flow * n / 60
                 n += 1
-                copies[k, mask].wait_recv()
+                if not merged:
+                    copies[k, mask].wait_recv()
+                elif k == 0:
+                    landed_all(half.gathered.at[pl.ds(0, STREAMS * PU)], half.ag_recv.at[mask - 1])
                 for s in range(last_step(mask) + 1, 4):
                     forward(k, mask, s)
 
@@ -521,7 +525,7 @@
         shared.work[:, :H] = shared.early_gram[...]
         shared.work[:, H:] = (i0 == i1).astype(F32)
         for n, _ in enumerate(eliminate(shared.work)):
-            yield eliminate_at + (0 if n < 12 else 4.2)
+            yield eliminate_at + (0 if n < 9 else 4.2)
         early_ref[:, :H] = jnp.where(i1 >= i0, shared.work[:, :H], 0.0)
         early_ref[:, H:] = jnp.where(i0 >= i1, shared.work[:, H:], 0.0)
 
@@ -574,7 +578,7 @@
 
     def second():
         yield 9.0
-        yield from gather(b, 13.2, 10.0)
+        yield from gather(b, 13.2, 10.0, merged=True)
         yield from multiply(b, True, b.gathered, b.part, 27.0, 0.36)
         yield from exchange(b, 34.0, (34.2, 42.6, 50.2, 57.0), 61.6, (64.5, 67.8, 71.2, 74.6), 77.4)
         yield from multiply(b, False, b.columns, b.part2, 78.0, 0.3)
@@ -599,7 +603,8 @@
 
 def iterate_call(tiles, rows, cols, count, sketch):
     smem = pl.BlockSpec(memory_space=pltpu.SMEM)
-    scratch = [make() for _ in range(2) for make in HALF_SCRATCH.values()]
+    scratch = [make() for make in HALF_SCRATCH.values()]
+    scratch += [dma(15) if name == "ag_recv" else make() for name, make in HALF_SCRATCH.items()]
     scratch += [make() for make in SHARED_SCRATCH.values()]
     return pl.pallas_call(
         iterate,

time: 142 us -> 143 us (level)
  no operation moved by 1% of the time
where the time goes in v6:
time: 143 us; the launch traced here: 142 us
  Pallas kernels  141 us (99%)
    pallas_call x1, Pallas kernels, iterate_call(): pl.pallas_call(iterate, out_shape=(jax.ShapeDtypeStruct((SHARD, K), F32),...  134 us
    pallas_call x1, Pallas kernels, factor_and_basis(): pl.pallas_call(factor_kernel, out_shape=(jax.ShapeDtypeStruct((SHARD, K),...  7.34 us

profile of v6, /device:TPU:1, one launch (start us, length us, event | category | flops | bytes accessed | tf_op | source)
XLA Modules:
  0.0 142.4 jit_solution(9455538960837415304)
XLA Ops:
  1.3 133.8 %iterate.1 = (f32[384,256]{1,0:T(8,128)}, f32[128,256]{1,0:T(8,128)}, f32[256,128]{1,0:T(8,128)}) custom-call(s32[16]{0:T(128)} %bitcast.6, s32[16]{0:T(128)} %bitcast.7, s32[1]{0:T(128)} %bitcast.4.count_ref, bf16[16,512,512]{2,1,0:T(8,128)(2,1)} %bitcast.5, bf16[384,256]{1,0:T(8,128)(2,1)} %sketch_ref.1), custom_call_target="tpu_custom_call" | custom-call | tf_op jit(solution)/shard_map/iterate/pallas_call | solution.py:609
  135.1 7.3 %factor.1 = (f32[384,256]{1,0:T(8,128)}, f32[256,256]{1,0:T(8,128)}) custom-call(f32[128,256]{1,0:T(8,128)} %get-tuple-element.5.early_ref, f32[256,128]{1,0:T(8,128)} %get-tuple-element.6.late_ref, f32[384,256]{1,0:T(8,128)} %get-tuple-element.7.ns_ref), custom_call_target="tpu_custom_call" | custom-call | tf_op jit(solution)/shard_map/factor/pallas_call | solution.py:646
